TPU v7x, 32 devices: a whole 2x2x4 slice. The times are simulated.
32 devices in a mesh: dp: 4 (over x, core), context: 4 (over z), tensor: 2 (over y).
Axes of the slice: x: 2, y: 2, z: 4, core: 2. Of those that a mesh axis runs over, the one named last changes fastest.
Arguments:
- tokens: bfloat16 [4, 1024, 1536], P('dp', 'context'), may hold values from -6 to 6
- lengths: int32 [4], P('dp'), may hold values from 256 to 1024, as said below
- gain_one: bfloat16 [1536], replicated, may hold values from 0.5 to 1.5
- w_query: bfloat16 [1536, 1536], P('dp', 'tensor'), may hold values from -0.15625 to 0.15625
- b_query: bfloat16 [1536], P('tensor'), may hold values from -3 to 3
- key_weight: bfloat16 [1536, 256], P('dp', 'tensor'), may hold values from -0.15625 to 0.15625
- key_bias: bfloat16 [256], P('tensor'), may hold values from -3 to 3
- value_weight: bfloat16 [1536, 256], P('dp', 'tensor'), may hold values from -0.15625 to 0.15625
- value_bias: bfloat16 [256], P('tensor'), may hold values from -3 to 3
- w_out: bfloat16 [1536, 1536], P('dp', 'tensor'), may hold values from -1.25 to 1.25
- gain_two: bfloat16 [1536], replicated, may hold values from 0.5 to 1.5
- w_gate: bfloat16 [1536, 8960], P('dp', 'tensor'), may hold values from -0.15625 to 0.15625
- w_up: bfloat16 [1536, 8960], P('dp', 'tensor'), may hold values from -0.15625 to 0.15625
- w_down: bfloat16 [1536, 8960], P('dp', 'tensor'), may hold values from -0.0625 to 0.0625
- grad_out: bfloat16 [4, 1024, 1536], P('dp', 'context'), may hold values from -6 to 6
Outputs:
- output: bfloat16 [4, 1024, 1536], P('dp', 'context')
- grad_tokens: bfloat16 [4, 1024, 1536], P('dp', 'context')
- grad_gain_one: float32 [1536], replicated
- grad_w_query: float32 [1536, 1536], P('dp', 'tensor')
- grad_b_query: float32 [1536], P('tensor')
- grad_w_key: float32 [1536, 256], P('dp', 'tensor')
- grad_b_key: float32 [256], P('tensor')
- grad_w_value: float32 [1536, 256], P('dp', 'tensor')
- grad_b_value: float32 [256], P('tensor')
- grad_w_out: float32 [1536, 1536], P('dp', 'tensor')
- grad_gain_two: float32 [1536], replicated
- grad_w_gate: float32 [1536, 8960], P('dp', 'tensor')
- grad_w_up: float32 [1536, 8960], P('dp', 'tensor')
- grad_w_down: float32 [1536, 8960], P('dp', 'tensor')
Inputs may be any that keep to these rules, and one draw needn't show every extreme that they name: `lengths`: each sequence's valid tokens fill its first slots; one sequence fills all 1024 slots and one holds exactly 256.
All inputs are finite; a program needn't handle non-finite values.
Results may differ from a plain program's by a relative error of at most 0.022.
Values may be sent and summed in bfloat16 or wider, within the bound.
A program may use at most 448 MiB of HBM per device.

v0:
```python
import math

import jax
import jax.numpy as jnp
from jax import lax
from jax.sharding import PartitionSpec as P

HEAD_DIM = 128


EPSILON = 1e-06
ROPE_BASE = 1000000.0


def shortened(value):
    return jax.tree.map(lambda a: a.astype(jnp.bfloat16) if a.dtype == jnp.float32 else a, value)


def collect(pieces):
    return jax.tree.map(
        lambda part, own: part.astype(own.dtype),
        lax.all_gather(shortened(pieces), "dp", axis=0, tiled=True),
        pieces,
    )


def branch_total(partial_value):
    return lax.psum(partial_value, "tensor")


def input_total(partial_value):
    return lax.psum(partial_value, "tensor")


def contract_last(left, right):
    return lax.dot_general(
        left, right, (((1,), (1,)), ((), ())), preferred_element_type=jnp.float32
    )


def contract_first(left, right):
    return lax.dot_general(
        left, right, (((0,), (0,)), ((), ())), preferred_element_type=jnp.float32
    )


def apply_rotation(field, cosine_rows, sine_table):
    half = field.shape[-1] // 2
    first = field[..., :half]
    second = field[..., half:]
    return jnp.concatenate(
        [first * cosine_rows - second * sine_table, second * cosine_rows + first * sine_table], -1
    )


def rotate_back(field, cosine_rows, sine_table):
    half = field.shape[-1] // 2
    first = field[..., :half]
    second = field[..., half:]
    return jnp.concatenate(
        [first * cosine_rows + second * sine_table, second * cosine_rows - first * sine_table], -1
    )


def norm_back(field, scale_rows, gain, d_normed):
    weighted = d_normed * gain
    cubed = scale_rows * scale_rows * scale_rows
    return scale_rows * weighted - field * cubed * jnp.mean(field * weighted, -1, keepdims=True)


def local(
    tokens,
    lengths,
    gain_one,
    w_query,
    b_query,
    key_weight,
    key_bias,
    value_weight,
    value_bias,
    w_out,
    gain_two,
    w_gate,
    w_up,
    w_down,
    grad_out,
):
    seq_count, block_len, model_width = tokens.shape
    row_count = seq_count * block_len
    head_count = w_query.shape[1] // HEAD_DIM
    kv_count = key_weight.shape[1] // HEAD_DIM
    query_group_width = head_count // kv_count
    position_count = block_len * lax.axis_size("context")
    positions = lax.axis_index("context") * block_len + jnp.arange(block_len, dtype=jnp.int32)
    key_places = jnp.arange(position_count, dtype=jnp.int32)
    valid_rows = (positions[None, :] < lengths[:, None]).astype(jnp.float32).reshape(row_count, 1)
    allowed = (key_places[None, None, :] <= positions[None, :, None]) & (
        key_places[None, None, :] < lengths[:, None, None]
    )
    allowed = allowed[:, None, None]
    half = HEAD_DIM // 2
    inverse = jnp.exp(jnp.arange(half, dtype=jnp.float32) * (-2.0 * math.log(ROPE_BASE) / HEAD_DIM))
    angles = positions.astype(jnp.float32)[:, None] * inverse[None, :]
    cosine_rows = jnp.tile(jnp.cos(angles)[:, None, :], (seq_count, 1, 1))
    sine_table = jnp.tile(jnp.sin(angles)[:, None, :], (seq_count, 1, 1))
    score_scale = 1.0 / math.sqrt(HEAD_DIM)
    gain_first = gain_one.astype(jnp.float32)
    gain_second = gain_two.astype(jnp.float32)
    inputs = tokens.reshape(row_count, model_width).astype(jnp.float32)
    scale_one = lax.rsqrt(jnp.mean(inputs * inputs, -1, keepdims=True) + EPSILON)
    normalized_input = (inputs * scale_one * gain_first).astype(jnp.bfloat16)
    full_query, full_key, full_value, full_out = collect((w_query, key_weight, value_weight, w_out))
    query_rows = jnp.dot(
        normalized_input, full_query, preferred_element_type=jnp.float32
    ) + b_query.astype(jnp.float32)
    keys_before_rotation = jnp.dot(
        normalized_input, full_key, preferred_element_type=jnp.float32
    ) + key_bias.astype(jnp.float32)
    values_pre = jnp.dot(
        normalized_input, full_value, preferred_element_type=jnp.float32
    ) + value_bias.astype(jnp.float32)
    query_rot = apply_rotation(
        query_rows.reshape(row_count, head_count, HEAD_DIM), cosine_rows, sine_table
    ).astype(jnp.bfloat16)
    key_rot = apply_rotation(
        keys_before_rotation.reshape(row_count, kv_count, HEAD_DIM), cosine_rows, sine_table
    ).astype(jnp.bfloat16)
    value_low = values_pre.astype(jnp.bfloat16)
    keys_all, values_all = (
        lax.all_gather(
            key_rot.reshape(seq_count, block_len, kv_count * HEAD_DIM),
            "context",
            axis=1,
            tiled=True,
        ),
        lax.all_gather(
            value_low.reshape(seq_count, block_len, kv_count * HEAD_DIM),
            "context",
            axis=1,
            tiled=True,
        ),
    )
    query_grid = query_rot.reshape(seq_count, block_len, kv_count, query_group_width, HEAD_DIM)
    key_grid = keys_all.reshape(seq_count, position_count, kv_count, HEAD_DIM)
    value_grid = values_all.reshape(seq_count, position_count, kv_count, HEAD_DIM)

    def masked_scores():
        raw = (
            jnp.einsum(
                "sqkgd,stkd->skgqt", query_grid, key_grid, preferred_element_type=jnp.float32
            )
            * score_scale
        )
        return jnp.where(allowed, raw, -1e30)

    scores = masked_scores()
    row_max = jnp.max(scores, -1, keepdims=True)
    exp_scores = jnp.exp(scores - row_max)
    row_sums = jnp.sum(exp_scores, -1, keepdims=True)
    logsum = row_max + jnp.log(row_sums)
    attention = (exp_scores / row_sums).astype(jnp.bfloat16)
    mixed_heads = jnp.einsum(
        "skgqt,stkd->sqkgd", attention, value_grid, preferred_element_type=jnp.float32
    )
    mixed_heads = mixed_heads.reshape(row_count, head_count * HEAD_DIM).astype(jnp.bfloat16)
    hidden = inputs + branch_total(contract_last(mixed_heads, full_out))
    scale_two = lax.rsqrt(jnp.mean(hidden * hidden, -1, keepdims=True) + EPSILON)
    normed_two = (hidden * scale_two * gain_second).astype(jnp.bfloat16)
    full_gate, full_up, full_down = collect((w_gate, w_up, w_down))
    gate_act = jnp.dot(normed_two, full_gate, preferred_element_type=jnp.float32)
    up_act = jnp.dot(normed_two, full_up, preferred_element_type=jnp.float32)
    sigmoid_gate = jax.nn.sigmoid(gate_act)
    swish_gate = gate_act * sigmoid_gate
    active = (swish_gate * up_act).astype(jnp.bfloat16)
    result = valid_rows * (hidden + branch_total(contract_last(active, full_down)))
    output = result.astype(jnp.bfloat16).reshape(seq_count, block_len, model_width)
    fall_grad = grad_out.reshape(row_count, model_width).astype(jnp.float32) * valid_rows
    fall_low = fall_grad.astype(jnp.bfloat16)
    back_gate, back_up, back_down = (full_gate, full_up, full_down)
    d_active = jnp.dot(fall_low, back_down, preferred_element_type=jnp.float32)
    d_gate = (d_active * up_act * sigmoid_gate * (1.0 + gate_act * (1.0 - sigmoid_gate))).astype(
        jnp.bfloat16
    )
    d_up = (d_active * swish_gate).astype(jnp.bfloat16)
    d_normed_two = input_total(contract_last(d_gate, back_gate) + contract_last(d_up, back_up))
    gain_two_grad = jnp.sum(d_normed_two * hidden * scale_two, 0)
    d_hidden = fall_grad + norm_back(hidden, scale_two, gain_second, d_normed_two)
    left = normed_two
    below = fall_low
    feed_share = lax.psum_scatter(
        jnp.concatenate(
            [
                contract_first(left, d_gate),
                contract_first(left, d_up),
                contract_first(below, active),
            ],
            1,
        ),
        "dp",
        scatter_dimension=0,
        tiled=True,
    )
    d_branch = d_hidden.astype(jnp.bfloat16)
    back_query, back_key, back_value, back_out = (full_query, full_key, full_value, full_out)
    d_mixed = jnp.dot(d_branch, back_out, preferred_element_type=jnp.float32).astype(jnp.bfloat16)
    mixed_grid = d_mixed.reshape(seq_count, block_len, kv_count, query_group_width, HEAD_DIM)
    scores = masked_scores()
    attention_full = jnp.exp(scores - logsum)
    attention = attention_full.astype(jnp.bfloat16)
    d_probs = jnp.einsum(
        "sqkgd,stkd->skgqt", mixed_grid, value_grid, preferred_element_type=jnp.float32
    )
    d_scores = (
        attention_full * (d_probs - jnp.sum(d_probs * attention_full, -1, keepdims=True))
    ).astype(jnp.bfloat16)
    d_query_rot = (
        jnp.einsum("skgqt,stkd->sqkgd", d_scores, key_grid, preferred_element_type=jnp.float32)
        * score_scale
    )
    d_keys_all = (
        jnp.einsum("skgqt,sqkgd->stkd", d_scores, query_grid, preferred_element_type=jnp.float32)
        * score_scale
    )
    d_values_all = jnp.einsum(
        "skgqt,sqkgd->stkd", attention, mixed_grid, preferred_element_type=jnp.float32
    )
    d_key_own, d_value_own = (
        lax.psum_scatter(
            d_keys_all.reshape(seq_count, position_count, kv_count * HEAD_DIM),
            "context",
            scatter_dimension=1,
            tiled=True,
        ),
        lax.psum_scatter(
            d_values_all.reshape(seq_count, position_count, kv_count * HEAD_DIM),
            "context",
            scatter_dimension=1,
            tiled=True,
        ),
    )
    d_query_low = (
        rotate_back(d_query_rot.reshape(row_count, head_count, HEAD_DIM), cosine_rows, sine_table)
        .reshape(row_count, head_count * HEAD_DIM)
        .astype(jnp.bfloat16)
    )
    d_key_low = (
        rotate_back(d_key_own.reshape(row_count, kv_count, HEAD_DIM), cosine_rows, sine_table)
        .reshape(row_count, kv_count * HEAD_DIM)
        .astype(jnp.bfloat16)
    )
    d_value_low = d_value_own.reshape(row_count, kv_count * HEAD_DIM).astype(jnp.bfloat16)
    d_normed = input_total(
        contract_last(d_query_low, back_query)
        + contract_last(d_key_low, back_key)
        + contract_last(d_value_low, back_value)
    )
    gain_one_grad = jnp.sum(d_normed * inputs * scale_one, 0)
    d_inputs = d_hidden + norm_back(inputs, scale_one, gain_first, d_normed)
    grad_tokens = d_inputs.astype(jnp.bfloat16).reshape(seq_count, block_len, model_width)
    small_sums = lax.psum(
        (
            gain_one_grad,
            gain_two_grad,
            jnp.sum(d_query_low.astype(jnp.float32), 0),
            jnp.sum(d_key_low.astype(jnp.float32), 0),
            jnp.sum(d_value_low.astype(jnp.float32), 0),
        ),
        ("dp", "context"),
    )
    left = normalized_input
    below = d_branch
    attention_share = lax.psum_scatter(
        jnp.concatenate(
            [
                contract_first(left, d_query_low),
                contract_first(left, d_key_low),
                contract_first(left, d_value_low),
                contract_first(below, mixed_heads),
            ],
            1,
        ),
        "dp",
        scatter_dimension=0,
        tiled=True,
    )
    feed_share, attention_share = lax.psum((feed_share, attention_share), "context")
    query_cols = w_query.shape[1]
    key_cols = key_weight.shape[1]
    unit_cols = w_gate.shape[1]
    return (
        output,
        grad_tokens,
        small_sums[0],
        attention_share[:, :query_cols],
        small_sums[2],
        attention_share[:, query_cols : query_cols + key_cols],
        small_sums[3],
        attention_share[:, query_cols + key_cols : query_cols + 2 * key_cols],
        small_sums[4],
        attention_share[:, query_cols + 2 * key_cols :],
        small_sums[1],
        feed_share[:, :unit_cols],
        feed_share[:, unit_cols : 2 * unit_cols],
        feed_share[:, 2 * unit_cols :],
    )


def solution(mesh):
    in_specs = (
        P("dp", "context", None),
        P("dp"),
        P(),
        P("dp", "tensor"),
        P("tensor"),
        P("dp", "tensor"),
        P("tensor"),
        P("dp", "tensor"),
        P("tensor"),
        P("dp", "tensor"),
        P(),
        P("dp", "tensor"),
        P("dp", "tensor"),
        P("dp", "tensor"),
        P("dp", "context", None),
    )
    out_specs = (
        P("dp", "context", None),
        P("dp", "context", None),
        P(),
        P("dp", "tensor"),
        P("tensor"),
        P("dp", "tensor"),
        P("tensor"),
        P("dp", "tensor"),
        P("tensor"),
        P("dp", "tensor"),
        P(),
        P("dp", "tensor"),
        P("dp", "tensor"),
        P("dp", "tensor"),
    )
    return jax.shard_map(local, mesh=mesh, in_specs=in_specs, out_specs=out_specs, check_vma=False)
```

profile of v0, /device:TPU:0, one launch (start us, length us, event | category | flops | bytes accessed | tf_op | source)
XLA Modules:
  0.0 2103.4 jit_solution(13525200338489626920)
XLA Ops:
  23.0 14.1 all_gather.30
  43.7 15.1 all-gather
  78.4 50.5 %all-reduce.8.cloned.1.call-done = f32[256,1536]{1,0:T(8,128)} async-done(((f32[256,1536]{1,0:T(8,128)}), f32[256,1536]{1,0:T(8,128)}) %all-reduce.8.cloned.1.call-update) | async-done | bytes 1572880 | tf_op jit(solution)/shard_map/psum | solution.py:28
  132.0 87.3 %all-gather.13.cloned.1.call-done = bf16[1536,4480]{1,0:T(8,128)(2,1)} async-done(((bf16[384,4480]{1,0:T(8,128)(2,1)}), bf16[1536,4480]{1,0:T(8,128)(2,1)}) %all-gather.13.cloned.1.call-update) | async-done | bytes 13762576 | tf_op jit(solution)/shard_map/all_gather | solution.py:22
  219.3 10.3 fusion.107
  229.6 80.0 %all-gather.11.cloned.1.call-done = bf16[1536,4480]{1,0:T(8,128)(2,1)} async-done(((bf16[384,4480]{1,0:T(8,128)(2,1)}), bf16[1536,4480]{1,0:T(8,128)(2,1)}) %all-gather.11.cloned.1.call-update) | async-done | bytes 13762576 | tf_op jit(solution)/shard_map/all_gather | solution.py:22
  309.6 10.3 fusion.106
  319.9 80.0 %all-gather.15.cloned.1.call-done = bf16[1536,4480]{1,0:T(8,128)(2,1)} async-done(((bf16[384,4480]{1,0:T(8,128)(2,1)}), bf16[1536,4480]{1,0:T(8,128)(2,1)}) %all-gather.15.cloned.1.call-update) | async-done | bytes 13762576 | tf_op jit(solution)/shard_map/all_gather | solution.py:22
  399.9 14.2 multiply_convert_fusion
  414.1 8.7 fusion.109
  422.9 8.5 convolution_add_fusion.2
  433.0 50.1 %all-reduce.10.cloned.1.call-done = f32[256,1536]{1,0:T(8,128)} async-done(((f32[256,1536]{1,0:T(8,128)}), f32[256,1536]{1,0:T(8,128)}) %all-reduce.10.cloned.1.call-update) | async-done | bytes 1572880 | tf_op jit(solution)/shard_map/psum | solution.py:32
  527.3 19.6 reduce-scatter.7.cloned.1.call-done
  548.2 9.3 pad_maximum_fusion.1
  558.0 17.2 fusion.112
  575.2 11.7 fusion.111
  586.9 11.6 fusion.51
  598.5 55.0 %pad_maximum_fusion = f32[1536,13440]{1,0:T(8,128)} fusion(f32[1536,4480]{1,0:T(8,128)} %fusion.51, f32[1536,4480]{1,0:T(8,128)} %fusion.112, f32[1536,4480]{1,0:T(8,128)} %fusion.111), kind=kLoop, calls=%fused_computation | loop fusion | flops 41287680 | bytes 165150720 | tf_op jit(solution)/shard_map/concatenate | solution.py:191
  653.6 11.6 fusion.108
  669.0 535.4 %reduce-scatter.11.cloned.1.call-done = f32[384,13440]{1,0:T(8,128)} async-done(((f32[1536,13440]{1,0:T(8,128)}), f32[384,13440]{1,0:T(8,128)}) %reduce-scatter.11.cloned.1.call-update) | async-done | bytes 20643856 | tf_op jit(solution)/shard_map/reduce_scatter | solution.py:190
  1204.8 88.6 %all-reduce.14.cloned.1.call-done = (f32[256,1536]{1,0:T(8,128)}, f32[256,1536]{1,0:T(8,128)}) async-done(((f32[256,1536]{1,0:T(8,128)}, f32[256,1536]{1,0:T(8,128)}), (f32[256,1536]{1,0:T(8,128)}, f32[256,1536]{1,0:T(8,128)})) %all-reduce.14.cloned.1.call-update) | async-done | bytes 3145744 | tf_op jit(solution)/shard_map/psum | solution.py:28
  1295.2 77.1 %all-reduce = (f32[1536]{0:T(1024)}, f32[768]{0:T(1024)}, f32[128]{0:T(128)}, f32[128]{0:T(128)}, f32[1536]{0:T(1024)}) all-reduce(f32[1536]{0:T(1024)S(1)} %get-tuple-element.44, f32[768]{0:T(1024)S(1)} %bitcast.206, f32[128]{0:T(128)S(1)} %convert_reduce_fusion.2, ...), channel_id=1, replica_groups=mesh['dp'=4,'context'=4,'tensor'=2] {'dp','context'}, use_global_device_ids=true, to_apply=%region_14.15 | all-reduce | flops 4096 | bytes 32768 | tf_op jit(solution)/shard_map/psum | solution.py:260
  1376.4 698.2 %all-reduce.12.cloned.1.call-done = (f32[384,1792]{0,1:T(8,128)}, f32[384,13440]{1,0:T(8,128)}) async-done(((f32[384,1792]{0,1:T(8,128)}, f32[384,13440]{1,0:T(8,128)}), (f32[384,1792]{0,1:T(8,128)}, f32[384,13440]{1,0:T(8,128)})) %all-reduce.12.cloned.1.call-update) | async-done | bytes 23396368 | tf_op jit(solution)/shard_map/psum | solution.py:286
  2077.4 14.8 fusion.100
  (204 shorter events, 108.6 us)
Async XLA Ops:
  7.2 29.9 %copy-start.34 = (bf16[384,128]{1,0:T(8,128)(2,1)S(1)}, bf16[384,128]{1,0:T(8,128)(2,1)}, u32[]{:S(2)}) copy-start(bf16[384,128]{1,0:T(8,128)(2,1)} %param.22) | copy-start | bytes 294916
  7.2 53.7 %all-gather.7.cloned.1.call-start = ((), (), s32[]{:S(2)}) async-start(), calls=%async_computation.4 | async-start | bytes 2949120 | tf_op jit(solution)/shard_map/all_gather | solution.py:22
  7.9 64.1 %all-gather.9.cloned.1.call-start = ((), (), s32[]{:S(2)}) async-start(), calls=%async_computation.5 | async-start | bytes 2949120 | tf_op jit(solution)/shard_map/all_gather | solution.py:22
  8.7 120.2 %all-reduce.8.cloned.1.call-start = ((), (), s32[]{:S(2)}) async-start(), calls=%async_computation.6 | async-start | bytes 3145728 | tf_op jit(solution)/shard_map/psum | solution.py:28
  8.7 50.0 %copy-start.47 = (f32[64]{0:T(128)}, f32[64]{0:T(128)S(1)}, u32[]{:S(2)}) copy-start(f32[64]{0:T(128)S(1)} %multiply_exponential_fusion) | copy-start | bytes 772
  10.7 48.0 %copy-start.45 = (f32[256]{0:T(256)}, f32[256]{0:T(256)S(1)}, u32[]{:S(2)}) copy-start(f32[256]{0:T(256)S(1)} %fusion.85) | copy-start | bytes 3076
  12.7 48.2 %copy-start.38 = (f32[256]{0:T(256)}, f32[256]{0:T(256)S(1)}, u32[]{:S(2)}) copy-start(f32[256]{0:T(256)S(1)} %get-tuple-element.82) | copy-start | bytes 3076
  22.2 21.5 %copy-start.20 = (bf16[1536,128]{1,0:T(8,128)(2,1)}, bf16[1536,128]{1,0:T(8,128)(2,1)S(1)}, u32[]{:S(2)}) copy-start(bf16[1536,128]{1,0:T(8,128)(2,1)S(1)} %all_gather.29) | copy-start | bytes 1179652
  37.1 28.4 %copy-start.14 = (bf16[1,1024,128]{1,2,0:T(8,128)(2,1)}, bf16[1,1024,128]{1,2,0:T(8,128)(2,1)S(1)}, u32[]{:S(2)}) copy-start(bf16[1,1024,128]{1,2,0:T(8,128)(2,1)S(1)} %all_gather.30) | copy-start | bytes 786436
  43.2 20.2 copy-start.22
  75.8 143.4 %all-gather.13.cloned.1.call-start = ((), (), s32[]{:S(2)}) async-start(), calls=%async_computation.8 | async-start | bytes 17203200 | tf_op jit(solution)/shard_map/all_gather | solution.py:22
  76.4 233.2 %all-gather.11.cloned.1.call-start = ((), (), s32[]{:S(2)}) async-start(), calls=%async_computation.7 | async-start | bytes 17203200 | tf_op jit(solution)/shard_map/all_gather | solution.py:22
  77.0 322.9 %all-gather.15.cloned.1.call-start = ((), (), s32[]{:S(2)}) async-start(), calls=%async_computation.9 | async-start | bytes 17203200 | tf_op jit(solution)/shard_map/all_gather | solution.py:22
  77.6 405.5 %all-reduce.10.cloned.1.call-start = ((), (), s32[]{:S(2)}) async-start(), calls=%async_computation.10 | async-start | bytes 3145728 | tf_op jit(solution)/shard_map/psum | solution.py:32
  431.4 92.7 %reduce-scatter.5.cloned.1.call-start = ((), (), s32[]{:S(2)}) async-start(), calls=%async_computation.11 | async-start | bytes 655360 | tf_op jit(solution)/shard_map/reduce_scatter | solution.py:228
  502.3 44.5 %reduce-scatter.7.cloned.1.call-start = ((), (), s32[]{:S(2)}) async-start(), calls=%async_computation.12 | async-start | bytes 655360 | tf_op jit(solution)/shard_map/reduce_scatter | solution.py:234
  513.9 155.2 %reduce-scatter.9.cloned.1.call-start = ((), (), s32[]{:S(2)}) async-start(), calls=%async_computation.13 | async-start | bytes 13762560 | tf_op jit(solution)/shard_map/reduce_scatter | solution.py:272
  557.5 646.9 %reduce-scatter.11.cloned.1.call-start = ((), (), s32[]{:S(2)}) async-start(), calls=%async_computation.14 | async-start | bytes 103219200 | tf_op jit(solution)/shard_map/reduce_scatter | solution.py:190
  558.0 17.2 copy-start.18
  653.5 639.9 %all-reduce.14.cloned.1.call-start = ((), (), s32[]{:S(2)}) async-start(), calls=%async_computation.16 | async-start | bytes 6291456 | tf_op jit(solution)/shard_map/psum | solution.py:28
  669.0 1405.6 %all-reduce.12.cloned.1.call-start = ((), (), s32[]{:S(2)}) async-start(), calls=%async_computation.15 | async-start | bytes 46792704 | tf_op jit(solution)/shard_map/psum | solution.py:286
  1204.5 90.7 %copy-start.41 = (f32[1536]{0:T(1024)S(1)}, f32[1536]{0:T(1024)}, u32[]{:S(2)}) copy-start(f32[1536]{0:T(1024)} %get-tuple-element.42) | copy-start | bytes 18436
  1204.5 90.7 %copy-start.44 = (f32[6,128]{1,0:T(8,128)S(1)}, f32[6,128]{1,0:T(8,128)}, u32[]{:S(2)}) copy-start(f32[6,128]{1,0:T(8,128)} %get-tuple-element.55) | copy-start | bytes 9220
  1295.2 79.8 %copy-start.48 = (f32[256]{0:T(256)S(1)}, f32[256]{0:T(256)}, u32[]{:S(2)}) copy-start(f32[256]{0:T(256)} %get-tuple-element.81) | copy-start | bytes 3076
  (42 other events, 172.4 us)
Sparse Core Ops, SparseCore 0:
  9.6 26.7 all-gather.6
  38.0 24.0 all-gather.8
  75.9 52.9 all-reduce.7
  130.4 88.7 all-gather.12
  220.7 88.7 all-gather.10
  311.1 88.7 all-gather.14
  431.5 51.4 all-reduce.9
  502.4 21.6 reduce-scatter.4
  527.0 19.8 reduce-scatter.6
  557.7 86.9 reduce-scatter.8
  653.6 550.7 reduce-scatter.10
  1207.4 85.9 all-reduce.13
  1296.0 778.5 all-reduce.11
where the time goes:
time: 2110 us; the launch traced here: 2100 us
  waiting for transfers between devices  1700 us (81%)
  matrix products  145 us (7%)
  blocking collectives  121 us (6%)
  other arithmetic  91.3 us (4%)
  local copies, waits for them, and re-layouts  33.8 us (2%)
    psum x1, waiting for transfers between devices, local(): lax.psum((feed_share, attention_share), 'context')  698 us
    reduce_scatter x1, waiting for transfers between devices, local(): lax.psum_scatter(jnp.concatenate([contract_first(left, d_gate), contract_...  535 us
    all_gather x5, waiting for transfers between devices, collect(): lax.all_gather(shortened(pieces), 'dp', axis=0, tiled=True)  247 us
    psum x2, waiting for transfers between devices, branch_total(): return lax.psum(partial_value, 'tensor')  139 us
    psum x1, blocking collectives, local(): lax.psum((gain_one_grad, gain_two_grad, jnp.sum(d_query_low.astype(jnp.fl...  77.1 us
    concatenate x1, other arithmetic, local(): jnp.concatenate([contract_first(left, d_gate), contract_first(left, d_up)...  55 us
    psum x1, waiting for transfers between devices, input_total(): return lax.psum(partial_value, 'tensor')  50.1 us
    dot_general x7, matrix products, contract_first(): lax.dot_general(left, right, (((0,), (0,)), ((), ())), preferred_element_...  49.9 us
  transfers between devices with their start and end apart: 13, of which 10 were waited for; matrix products, arithmetic and copies ran while one was open for 8% of the time, Pallas kernels for 0%

commit v1 on v0

v1 whole, which is shorter than its diff:
```python
import math

import jax
import jax.numpy as jnp
from jax import lax
from jax.sharding import PartitionSpec as P

HEAD_DIM = 128


EPSILON = 1e-06
ROPE_BASE = 1000000.0


def xor_pairs(size, mask):
    return [(i, i ^ mask) for i in range(size)]


def far_masks(size):
    masks, mask = [], 2
    while mask < size:
        masks.append(mask)
        mask *= 2
    return masks


def swap_blocks(blocks, me):
    mask = 1
    while mask < len(blocks):
        flag = (me & mask) != 0
        blocks = [jnp.where(flag, blocks[r ^ mask], blocks[r]) for r in range(len(blocks))]
        mask *= 2
    return blocks


def far_half(piece, mask, size, parity):
    half = piece.shape[0] // 2
    sent = lax.dynamic_slice_in_dim(piece, half * parity, half, 0)
    straight = lax.ppermute(sent, "dp", xor_pairs(size, mask))
    other = lax.ppermute(straight, "context", xor_pairs(lax.axis_size("context"), 1))
    first = jnp.where(parity == 0, straight, other)
    second = jnp.where(parity == 0, other, straight)
    return jnp.concatenate([first, second], 0)


def gather_pieces(own, size, parity=None):
    pieces = {0: own}
    for mask in far_masks(size):
        for r in list(pieces):
            if parity is None:
                pieces[r ^ mask] = lax.ppermute(pieces[r], "dp", xor_pairs(size, mask))
            else:
                pieces[r ^ mask] = far_half(pieces[r], mask, size, parity)
    if size > 1:
        for r in list(pieces):
            pieces[r ^ 1] = lax.ppermute(pieces[r], "dp", xor_pairs(size, 1))
    return [pieces[r] for r in range(size)]


def trade_blocks(blocks, size):
    return [blocks[0]] + [
        lax.ppermute(blocks[r], "dp", xor_pairs(size, r)) for r in range(1, size)
    ]


def tensor_sum(part):
    sent = part.astype(jnp.bfloat16)
    size = lax.axis_size("tensor")
    if size == 2:
        other = lax.ppermute(sent, "tensor", [(0, 1), (1, 0)])
        return sent.astype(jnp.float32) + other.astype(jnp.float32)
    return lax.psum(part, "tensor")


def line_sum(part):
    place = lax.axis_index("context")
    if lax.axis_size("context") != 4:
        return lax.psum(part.astype(jnp.float32), "context")
    got = lax.ppermute(part, "context", [(0, 1), (3, 2)])
    pair = (part.astype(jnp.float32) + got.astype(jnp.float32)).astype(jnp.bfloat16)
    got = lax.ppermute(pair, "context", [(1, 2), (2, 1)])
    total = (pair.astype(jnp.float32) + got.astype(jnp.float32)).astype(jnp.bfloat16)
    got = lax.ppermute(total, "context", [(1, 0), (2, 3)])
    ends = (place == 0) | (place == 3)
    return jnp.where(ends, got, total).astype(jnp.float32)


def small_total(vector):
    for axis in ("dp", "context"):
        size, mask = lax.axis_size(axis), 1
        while mask < size:
            vector = vector + lax.ppermute(vector, axis, xor_pairs(size, mask))
            mask *= 2
    return vector


def contract_last(left, right):
    return lax.dot_general(
        left, right, (((1,), (1,)), ((), ())), preferred_element_type=jnp.float32
    )


def contract_first(left, right):
    return lax.dot_general(
        left, right, (((0,), (0,)), ((), ())), preferred_element_type=jnp.float32
    )


def apply_rotation(field, cosine_rows, sine_table):
    half = field.shape[-1] // 2
    first = field[..., :half]
    second = field[..., half:]
    return jnp.concatenate(
        [first * cosine_rows - second * sine_table, second * cosine_rows + first * sine_table], -1
    )


def rotate_back(field, cosine_rows, sine_table):
    half = field.shape[-1] // 2
    first = field[..., :half]
    second = field[..., half:]
    return jnp.concatenate(
        [first * cosine_rows + second * sine_table, second * cosine_rows - first * sine_table], -1
    )


def norm_back(field, scale_rows, gain, d_normed):
    weighted = d_normed * gain
    cubed = scale_rows * scale_rows * scale_rows
    return scale_rows * weighted - field * cubed * jnp.mean(field * weighted, -1, keepdims=True)


def chunk_edges(columns):
    tiles = columns // 128
    count = next((n for n in (5, 4, 7, 6, 3, 2) if tiles % n == 0), 1)
    width = columns // count
    return [(n * width, width) for n in range(count)]


def local(
    tokens,
    lengths,
    gain_one,
    w_query,
    b_query,
    key_weight,
    key_bias,
    value_weight,
    value_bias,
    w_out,
    gain_two,
    w_gate,
    w_up,
    w_down,
    grad_out,
):
    bf16, f32 = jnp.bfloat16, jnp.float32
    seq_count, block_len, model_width = tokens.shape
    row_count = seq_count * block_len
    query_cols = w_query.shape[1]
    key_cols = key_weight.shape[1]
    unit_cols = w_gate.shape[1]
    own_rows = w_query.shape[0]
    head_count = query_cols // HEAD_DIM
    kv_count = key_cols // HEAD_DIM
    query_group_width = head_count // kv_count
    size = lax.axis_size("dp")
    me = lax.axis_index("dp")
    blocks_along = lax.axis_size("context")
    place = lax.axis_index("context")
    parity = place % 2 if blocks_along % 2 == 0 and own_rows % 32 == 0 else None

    def relative(field):
        return swap_blocks([field[:, n * own_rows : (n + 1) * own_rows] for n in range(size)], me)

    def absolute(blocks):
        return jnp.concatenate(swap_blocks(blocks, me), 1)

    def dot_rows(blocks, weights):
        return jnp.dot(
            jnp.concatenate(blocks, 1), jnp.concatenate(weights, 0), preferred_element_type=f32
        )

    attention_weights = gather_pieces(
        jnp.concatenate([w_query, key_weight, value_weight], 1), size
    )
    out_weights = gather_pieces(w_out, size, parity)
    edges = chunk_edges(unit_cols)
    feed_weights = []
    for start, width in edges:
        own = jnp.concatenate(
            [w[:, start : start + width] for w in (w_gate, w_up, w_down)], 1
        )
        feed_weights.append(gather_pieces(own, size, parity))

    positions = place * block_len + jnp.arange(block_len, dtype=jnp.int32)
    key_places = jnp.concatenate(
        [
            (place - shift) * block_len + jnp.arange(block_len, dtype=jnp.int32)
            for shift in range(blocks_along)
        ]
    )
    position_count = block_len * blocks_along
    valid_rows = (positions[None, :] < lengths[:, None]).astype(f32).reshape(row_count, 1)
    allowed = (
        (key_places[None, None, :] <= positions[None, :, None])
        & (key_places[None, None, :] < lengths[:, None, None])
        & (key_places[None, None, :] >= 0)
    )
    allowed = allowed[:, None, None]
    half = HEAD_DIM // 2
    inverse = jnp.exp(jnp.arange(half, dtype=f32) * (-2.0 * math.log(ROPE_BASE) / HEAD_DIM))
    angles = positions.astype(f32)[:, None] * inverse[None, :]
    cosine_rows = jnp.tile(jnp.cos(angles)[:, None, :], (seq_count, 1, 1))
    sine_table = jnp.tile(jnp.sin(angles)[:, None, :], (seq_count, 1, 1))
    score_scale = 1.0 / math.sqrt(HEAD_DIM)
    gain_first = gain_one.astype(f32)
    gain_second = gain_two.astype(f32)
    inputs = tokens.reshape(row_count, model_width).astype(f32)
    scale_one = lax.rsqrt(jnp.mean(inputs * inputs, -1, keepdims=True) + EPSILON)
    normalized_input = (inputs * scale_one * gain_first).astype(bf16)
    normed_blocks = relative(normalized_input)
    projected = dot_rows(normed_blocks, attention_weights)
    query_rows = projected[:, :query_cols] + b_query.astype(f32)
    keys_before_rotation = projected[:, query_cols : query_cols + key_cols] + key_bias.astype(f32)
    values_pre = projected[:, query_cols + key_cols :] + value_bias.astype(f32)
    query_rot = apply_rotation(
        query_rows.reshape(row_count, head_count, HEAD_DIM), cosine_rows, sine_table
    ).astype(bf16)
    key_rot = apply_rotation(
        keys_before_rotation.reshape(row_count, kv_count, HEAD_DIM), cosine_rows, sine_table
    ).astype(bf16)
    value_low = values_pre.astype(bf16)
    pair_rows = jnp.concatenate(
        [key_rot.reshape(seq_count, block_len, key_cols), value_low.reshape(seq_count, block_len, key_cols)], 2
    )
    pair_all = [pair_rows]
    for shift in range(1, blocks_along):
        pair_all.append(
            lax.ppermute(
                pair_rows, "context", [(n, n + shift) for n in range(blocks_along - shift)]
            )
        )
    pair_all = jnp.concatenate(pair_all, 1)
    query_grid = query_rot.reshape(seq_count, block_len, kv_count, query_group_width, HEAD_DIM)
    key_grid = pair_all[:, :, :key_cols].reshape(seq_count, position_count, kv_count, HEAD_DIM)
    value_grid = pair_all[:, :, key_cols:].reshape(seq_count, position_count, kv_count, HEAD_DIM)

    def masked_scores():
        raw = (
            jnp.einsum(
                "sqkgd,stkd->skgqt", query_grid, key_grid, preferred_element_type=f32
            )
            * score_scale
        )
        return jnp.where(allowed, raw, -1e30)

    scores = masked_scores()
    row_max = jnp.max(scores, -1, keepdims=True)
    exp_scores = jnp.exp(scores - row_max)
    row_sums = jnp.sum(exp_scores, -1, keepdims=True)
    logsum = row_max + jnp.log(row_sums)
    attention = (exp_scores / row_sums).astype(bf16)
    mixed_heads = jnp.einsum(
        "skgqt,stkd->sqkgd", attention, value_grid, preferred_element_type=f32
    )
    mixed_heads = mixed_heads.reshape(row_count, head_count * HEAD_DIM).astype(bf16)
    full_out = jnp.concatenate(out_weights, 0)
    branch = contract_last(mixed_heads, full_out)
    branch = absolute([branch[:, r * own_rows : (r + 1) * own_rows] for r in range(size)])
    hidden = inputs + tensor_sum(branch)
    scale_two = lax.rsqrt(jnp.mean(hidden * hidden, -1, keepdims=True) + EPSILON)
    normed_two = (hidden * scale_two * gain_second).astype(bf16)
    fall_grad = grad_out.reshape(row_count, model_width).astype(f32) * valid_rows
    fall_low = fall_grad.astype(bf16)
    fall_blocks = relative(fall_low)
    two_blocks = relative(normed_two)
    traded_early = trade_blocks(
        [jnp.concatenate([a, b], 1) for a, b in zip(normed_blocks, fall_blocks)], size
    )
    traded_early = jnp.concatenate(traded_early, 0)
    normed_features, fall_features = traded_early[:, :own_rows], traded_early[:, own_rows:]
    two_features = jnp.concatenate(trade_blocks(two_blocks, size), 0)

    feed_out = 0.0
    d_normed_two = 0.0
    feed_grads = []
    for (start, width), pieces in zip(edges, feed_weights):
        stacked = jnp.concatenate(pieces, 0)
        gate_part, up_part, down_part = (
            stacked[:, :width],
            stacked[:, width : 2 * width],
            stacked[:, 2 * width :],
        )
        two_row = jnp.concatenate(two_blocks, 1)
        fall_row = jnp.concatenate(fall_blocks, 1)
        gate_act = jnp.dot(two_row, gate_part, preferred_element_type=f32)
        up_act = jnp.dot(two_row, up_part, preferred_element_type=f32)
        d_active = jnp.dot(fall_row, down_part, preferred_element_type=f32)
        sigmoid_gate = jax.nn.sigmoid(gate_act)
        swish_gate = gate_act * sigmoid_gate
        active = (swish_gate * up_act).astype(bf16)
        d_gate = (
            d_active * up_act * sigmoid_gate * (1.0 + gate_act * (1.0 - sigmoid_gate))
        ).astype(bf16)
        d_up = (d_active * swish_gate).astype(bf16)
        feed_out = feed_out + contract_last(active, down_part)
        d_normed_two = (
            d_normed_two + contract_last(d_gate, gate_part) + contract_last(d_up, up_part)
        )
        acts = jnp.concatenate(
            gather_pieces(jnp.concatenate([d_gate, d_up, active], 1), size), 0
        )
        part = jnp.concatenate(
            [
                contract_first(two_features, acts[:, : 2 * width]),
                contract_first(fall_features, acts[:, 2 * width :]),
            ],
            1,
        ).astype(bf16)
        feed_grads.append(line_sum(part))

    def split(field):
        return [field[:, r * own_rows : (r + 1) * own_rows] for r in range(size)]

    d_normed_two = tensor_sum(absolute(split(d_normed_two)))
    result = valid_rows * (hidden + tensor_sum(absolute(split(feed_out))))
    output = result.astype(bf16).reshape(seq_count, block_len, model_width)
    gain_two_grad = jnp.sum(d_normed_two * hidden * scale_two, 0)
    d_hidden = fall_grad + norm_back(hidden, scale_two, gain_second, d_normed_two)
    d_branch = d_hidden.astype(bf16)
    branch_blocks = relative(d_branch)
    branch_features = jnp.concatenate(trade_blocks(branch_blocks, size), 0)
    d_mixed = jnp.dot(
        jnp.concatenate(branch_blocks, 1), full_out, preferred_element_type=f32
    ).astype(bf16)
    mixed_grid = d_mixed.reshape(seq_count, block_len, kv_count, query_group_width, HEAD_DIM)
    scores = masked_scores()
    attention_full = jnp.exp(scores - logsum)
    attention = attention_full.astype(bf16)
    d_probs = jnp.einsum(
        "sqkgd,stkd->skgqt", mixed_grid, value_grid, preferred_element_type=f32
    )
    d_scores = (
        attention_full * (d_probs - jnp.sum(d_probs * attention_full, -1, keepdims=True))
    ).astype(bf16)
    d_query_rot = (
        jnp.einsum("skgqt,stkd->sqkgd", d_scores, key_grid, preferred_element_type=f32)
        * score_scale
    )
    d_keys_all = (
        jnp.einsum("skgqt,sqkgd->stkd", d_scores, query_grid, preferred_element_type=f32)
        * score_scale
    )
    d_values_all = jnp.einsum(
        "skgqt,sqkgd->stkd", attention, mixed_grid, preferred_element_type=f32
    )
    d_pair = jnp.concatenate(
        [
            d_keys_all.reshape(seq_count, position_count, key_cols),
            d_values_all.reshape(seq_count, position_count, key_cols),
        ],
        2,
    )
    d_own = d_pair[:, :block_len]
    for shift in range(1, blocks_along):
        sent = d_pair[:, shift * block_len : (shift + 1) * block_len].astype(bf16)
        d_own = d_own + lax.ppermute(
            sent, "context", [(n, n - shift) for n in range(shift, blocks_along)]
        ).astype(f32)
    d_own = d_own.reshape(row_count, 2 * key_cols)
    d_query_low = (
        rotate_back(d_query_rot.reshape(row_count, head_count, HEAD_DIM), cosine_rows, sine_table)
        .reshape(row_count, head_count * HEAD_DIM)
        .astype(bf16)
    )
    d_key_low = (
        rotate_back(
            d_own[:, :key_cols].reshape(row_count, kv_count, HEAD_DIM), cosine_rows, sine_table
        )
        .reshape(row_count, key_cols)
        .astype(bf16)
    )
    d_value_low = d_own[:, key_cols:].astype(bf16)
    d_projected = jnp.concatenate([d_query_low, d_key_low, d_value_low], 1)
    d_normed = contract_last(d_projected, jnp.concatenate(attention_weights, 0))
    d_normed = tensor_sum(absolute(split(d_normed)))
    gain_one_grad = jnp.sum(d_normed * inputs * scale_one, 0)
    d_inputs = d_hidden + norm_back(inputs, scale_one, gain_first, d_normed)
    grad_tokens = d_inputs.astype(bf16).reshape(seq_count, block_len, model_width)
    gain_two_grad = small_total(gain_two_grad)
    small = small_total(
        jnp.concatenate([gain_one_grad, jnp.sum(d_projected.astype(f32), 0)])
    )
    mixed_all = jnp.concatenate(gather_pieces(mixed_heads, size), 0)
    out_grad = line_sum(contract_first(branch_features, mixed_all).astype(bf16))
    projected_all = jnp.concatenate(gather_pieces(d_projected, size), 0)
    projected_grad = line_sum(contract_first(normed_features, projected_all).astype(bf16))

    def columns(which):
        return jnp.concatenate(
            [g[:, which * w : (which + 1) * w] for g, (_, w) in zip(feed_grads, edges)], 1
        )

    low, high = model_width + query_cols, model_width + query_cols + key_cols
    return (
        output,
        grad_tokens,
        small[:model_width],
        projected_grad[:, :query_cols],
        small[model_width:low],
        projected_grad[:, query_cols : query_cols + key_cols],
        small[low:high],
        projected_grad[:, query_cols + key_cols :],
        small[high:],
        out_grad,
        gain_two_grad,
        columns(0),
        columns(1),
        columns(2),
    )


def solution(mesh):
    in_specs = (
        P("dp", "context", None),
        P("dp"),
        P(),
        P("dp", "tensor"),
        P("tensor"),
        P("dp", "tensor"),
        P("tensor"),
        P("dp", "tensor"),
        P("tensor"),
        P("dp", "tensor"),
        P(),
        P("dp", "tensor"),
        P("dp", "tensor"),
        P("dp", "tensor"),
        P("dp", "context", None),
    )
    out_specs = (
        P("dp", "context", None),
        P("dp", "context", None),
        P(),
        P("dp", "tensor"),
        P("tensor"),
        P("dp", "tensor"),
        P("tensor"),
        P("dp", "tensor"),
        P("tensor"),
        P("dp", "tensor"),
        P(),
        P("dp", "tensor"),
        P("dp", "tensor"),
        P("dp", "tensor"),
    )
    return jax.shard_map(local, mesh=mesh, in_specs=in_specs, out_specs=out_specs, check_vma=False)
```

time: 2110 us -> 1080 us (0.51)
  waiting for transfers between devices: 1700 us -> 678 us
  blocking collectives: 121 us -> 0 us
  starting transfers between devices: 1.31 us -> 97.5 us
  matrix products: 145 us -> 95.7 us
  local copies, waits for them, and re-layouts: 33.8 us -> 80 us
  other arithmetic: 91.3 us -> 114 us
    psum x4 -> x0, waiting for transfers between devices: 887 us -> none  [the longest x1 698 us: local(): lax.psum((feed_share, attention_share), 'context')]
    ppermute x0 -> x96, waiting for transfers between devices: none -> 678 us  [the longest x7 224 us: line_sum(): got = lax.ppermute(total, 'context', [(1, 0), (2, 3)])]
    reduce_scatter x4 -> x0, waiting for transfers between devices: 558 us -> none  [the longest x1 535 us: local(): lax.psum_scatter(jnp.concatenate([contract_first(left, d_gate), contract_...]
    all_gather x5 -> x0, waiting for transfers between devices: 247 us -> none  [collect(): lax.all_gather(shortened(pieces), 'dp', axis=0, tiled=True)]
    ppermute x0 -> x96, starting transfers between devices: none -> 97.5 us  [the longest x7 21.7 us: line_sum(): got = lax.ppermute(part, 'context', [(0, 1), (3, 2)])]
    psum x1 -> x0, blocking collectives: 77.1 us -> none  [local(): lax.psum((gain_one_grad, gain_two_grad, jnp.sum(d_query_low.astype(jnp.fl...]
    all_gather x4 -> x0, blocking collectives: 43.4 us -> none  [the longest x1 15.1 us: local(): lax.all_gather(value_low.reshape(seq_count, block_len, kv_count * HEAD_DI...]
    unnamed x112 -> x301, local copies, waits for them, and re-layouts: 12.7 us -> 49.5 us
  transfers between devices with their start and end apart: 13 -> 96, of which waited for: 10 -> 34; matrix products, arithmetic and copies ran while one was open for 8% -> 24% of each run, Pallas kernels for 0% -> 0%
where the time goes in v1:
time: 1080 us; the launch traced here: 1070 us
  waiting for transfers between devices  678 us (63%)
  other arithmetic  114 us (11%)
  starting transfers between devices  97.5 us (9%)
  matrix products  95.7 us (9%)
  local copies, waits for them, and re-layouts  80 us (7%)
    ppermute x7, waiting for transfers between devices, line_sum(): got = lax.ppermute(total, 'context', [(1, 0), (2, 3)])  224 us
    ppermute x7, waiting for transfers between devices, line_sum(): got = lax.ppermute(part, 'context', [(0, 1), (3, 2)])  170 us
    ppermute x6, waiting for transfers between devices, far_half(): lax.ppermute(straight, 'context', xor_pairs(lax.axis_size('context'), 1))  53.8 us
    ppermute x6, waiting for transfers between devices, far_half(): straight = lax.ppermute(sent, 'dp', xor_pairs(size, mask))  50.1 us
    unnamed x301, local copies, waits for them, and re-layouts  49.5 us
    ppermute x9, waiting for transfers between devices, trade_blocks(): lax.ppermute(blocks[r], 'dp', xor_pairs(size, r))  46.8 us
    concatenate x5, other arithmetic, local(): jnp.concatenate(gather_pieces(jnp.concatenate([d_gate, d_up, active], 1),...  43.5 us
    ppermute x8, waiting for transfers between devices, gather_pieces(): pieces[r ^ mask] = lax.ppermute(pieces[r], 'dp', xor_pairs(size, mask))  41.9 us
  transfers between devices with their start and end apart: 96, of which 34 were waited for; matrix products, arithmetic and copies ran while one was open for 24% of the time, Pallas kernels for 0%

profile of v1, /device:TPU:0, one launch (start us, length us, event | category | flops | bytes accessed | tf_op | source)
XLA Modules:
  0.0 1069.3 jit_solution(7971990309310454799)
XLA Ops:
  104.1 10.8 %collective-permute-done.20 = bf16[192,2688]{1,0:T(8,128)(2,1)S(1)} collective-permute-done((bf16[192,2688]{1,0:T(8,128)(2,1)}, bf16[192,2688]{1,0:T(8,128)(2,1)S(1)}, u32[]{:S(2)}, u32[]{:S(2)}) %collective-permute-start.20) | collective-permute-done | bytes 1032224 | tf_op jit(solution)/shard_map/ppermute | solution.py:39
  121.1 18.3 %collective-permute-done.21 = bf16[192,2688]{1,0:T(8,128)(2,1)S(1)} collective-permute-done((bf16[192,2688]{1,0:T(8,128)(2,1)S(1)}, bf16[192,2688]{1,0:T(8,128)(2,1)S(1)}, u32[]{:S(2)}, u32[]{:S(2)}) %collective-permute-start.21) | collective-permute-done | bytes 1032224 | tf_op jit(solution)/shard_map/ppermute | solution.py:40
  141.2 17.9 %collective-permute-done.28 = bf16[192,2688]{1,0:T(8,128)(2,1)S(1)} collective-permute-done((bf16[192,2688]{1,0:T(8,128)(2,1)S(1)}, bf16[192,2688]{1,0:T(8,128)(2,1)S(1)}, u32[]{:S(2)}, u32[]{:S(2)}) %collective-permute-start.28) | collective-permute-done | bytes 1032224 | tf_op jit(solution)/shard_map/ppermute | solution.py:39
  159.1 21.4 %collective-permute-done.24 = bf16[192,2688]{1,0:T(8,128)(2,1)S(1)} collective-permute-done((bf16[192,2688]{1,0:T(8,128)(2,1)S(1)}, bf16[192,2688]{1,0:T(8,128)(2,1)S(1)}, u32[]{:S(2)}, u32[]{:S(2)}) %collective-permute-start.24) | collective-permute-done | bytes 1032224 | tf_op jit(solution)/shard_map/ppermute | solution.py:39
  191.2 15.0 %collective-permute-done.29 = bf16[192,2688]{1,0:T(8,128)(2,1)S(1)} collective-permute-done((bf16[192,2688]{1,0:T(8,128)(2,1)S(1)}, bf16[192,2688]{1,0:T(8,128)(2,1)S(1)}, u32[]{:S(2)}, u32[]{:S(2)}) %collective-permute-start.29) | collective-permute-done | bytes 1032224 | tf_op jit(solution)/shard_map/ppermute | solution.py:40
  211.8 14.9 %collective-permute-done.25 = bf16[192,2688]{1,0:T(8,128)(2,1)S(1)} collective-permute-done((bf16[192,2688]{1,0:T(8,128)(2,1)S(1)}, bf16[192,2688]{1,0:T(8,128)(2,1)S(1)}, u32[]{:S(2)}, u32[]{:S(2)}) %collective-permute-start.25) | collective-permute-done | bytes 1032224 | tf_op jit(solution)/shard_map/ppermute | solution.py:40
  300.0 15.8 %collective-permute-done.32 = bf16[256,1536]{1,0:T(8,128)(2,1)S(1)} collective-permute-done((bf16[256,1536]{1,0:T(8,128)(2,1)S(1)}, bf16[256,1536]{1,0:T(8,128)(2,1)S(1)}, u32[]{:S(2)}, u32[]{:S(2)}) %collective-permute-start.32) | collective-permute-done | bytes 786464 | tf_op jit(solution)/shard_map/ppermute | solution.py:70
  316.5 15.4 %collective-permute-done.31 = bf16[256,1536]{1,0:T(8,128)(2,1)S(1)} collective-permute-done((bf16[256,1536]{1,0:T(8,128)(2,1)S(1)}, bf16[256,1536]{1,0:T(8,128)(2,1)S(1)}, u32[]{:S(2)}, u32[]{:S(2)}) %collective-permute-start.31) | collective-permute-done | bytes 786464 | tf_op jit(solution)/shard_map/ppermute | solution.py:70
  405.7 34.1 %collective-permute-done.38 = f32[2560]{0:T(1024)S(1)} collective-permute-done((f32[2560]{0:T(1024)S(1)}, f32[2560]{0:T(1024)S(1)}, u32[]{:S(2)}, u32[]{:S(2)}) %collective-permute-start.38) | collective-permute-done | bytes 10272 | tf_op jit(solution)/shard_map/ppermute | solution.py:92
  460.7 13.6 %collective-permute-done.79 = bf16[256,2688]{1,0:T(8,128)(2,1)S(1)} collective-permute-done((bf16[256,2688]{1,0:T(8,128)(2,1)S(1)}, bf16[256,2688]{1,0:T(8,128)(2,1)S(1)}, u32[]{:S(2)}, u32[]{:S(2)}) %collective-permute-start.79) | collective-permute-done | bytes 1376288 | tf_op jit(solution)/shard_map/ppermute | solution.py:51
  475.1 28.3 %collective-permute-done.73 = bf16[256,2688]{1,0:T(8,128)(2,1)S(1)} collective-permute-done((bf16[256,2688]{1,0:T(8,128)(2,1)S(1)}, bf16[256,2688]{1,0:T(8,128)(2,1)S(1)}, u32[]{:S(2)}, u32[]{:S(2)}) %collective-permute-start.73) | collective-permute-done | bytes 1376288 | tf_op jit(solution)/shard_map/ppermute | solution.py:51
  526.1 9.4 pad_maximum_fusion.1
  537.7 42.2 %collective-permute-done.64 = bf16[256,384]{1,0:T(8,128)(2,1)S(1)} collective-permute-done((bf16[256,384]{1,0:T(8,128)(2,1)S(1)}, bf16[256,384]{1,0:T(8,128)(2,1)S(1)}, u32[]{:S(2)}, u32[]{:S(2)}) %collective-permute-start.64) | collective-permute-done | bytes 196640 | tf_op jit(solution)/shard_map/ppermute | solution.py:62
  591.1 12.6 %collective-permute-done.47 = bf16[384,1024]{1,0:T(8,128)(2,1)S(1)} collective-permute-done((bf16[384,1024]{1,0:T(8,128)(2,1)}, bf16[384,1024]{1,0:T(8,128)(2,1)S(1)}, u32[]{:S(2)}, u32[]{:S(2)}) %collective-permute-start.47) | collective-permute-done | bytes 786464 | tf_op jit(solution)/shard_map/ppermute | solution.py:79
  614.6 9.3 pad_maximum_fusion.4
  654.4 11.8 %collective-permute-done.49 = bf16[384,1024]{1,0:T(8,128)(2,1)S(1)} collective-permute-done((bf16[384,1024]{1,0:T(8,128)(2,1)S(1)}, bf16[384,1024]{1,0:T(8,128)(2,1)S(1)}, u32[]{:S(2)}, u32[]{:S(2)}) %collective-permute-start.49) | collective-permute-done | bytes 786464 | tf_op jit(solution)/shard_map/ppermute | solution.py:83
  671.4 30.1 %collective-permute-done.81 = bf16[384,2688]{1,0:T(8,128)(2,1)S(1)} collective-permute-done((bf16[384,2688]{1,0:T(8,128)(2,1)S(1)}, bf16[384,2688]{1,0:T(8,128)(2,1)S(1)}, u32[]{:S(2)}, u32[]{:S(2)}) %collective-permute-start.81) | collective-permute-done | bytes 2064416 | tf_op jit(solution)/shard_map/ppermute | solution.py:79
  702.9 42.9 %collective-permute-done.75 = bf16[384,2688]{1,0:T(8,128)(2,1)S(1)} collective-permute-done((bf16[384,2688]{1,0:T(8,128)(2,1)S(1)}, bf16[384,2688]{1,0:T(8,128)(2,1)S(1)}, u32[]{:S(2)}, u32[]{:S(2)}) %collective-permute-start.75) | collective-permute-done | bytes 2064416 | tf_op jit(solution)/shard_map/ppermute | solution.py:79
  747.1 42.9 %collective-permute-done.93 = bf16[384,2688]{1,0:T(8,128)(2,1)S(1)} collective-permute-done((bf16[384,2688]{1,0:T(8,128)(2,1)S(1)}, bf16[384,2688]{1,0:T(8,128)(2,1)S(1)}, u32[]{:S(2)}, u32[]{:S(2)}) %collective-permute-start.93) | collective-permute-done | bytes 2064416 | tf_op jit(solution)/shard_map/ppermute | solution.py:79
  791.3 41.6 %collective-permute-done.87 = bf16[384,2688]{1,0:T(8,128)(2,1)S(1)} collective-permute-done((bf16[384,2688]{1,0:T(8,128)(2,1)S(1)}, bf16[384,2688]{1,0:T(8,128)(2,1)S(1)}, u32[]{:S(2)}, u32[]{:S(2)}) %collective-permute-start.87) | collective-permute-done | bytes 2064416 | tf_op jit(solution)/shard_map/ppermute | solution.py:79
  843.2 43.7 %collective-permute-done.71 = bf16[384,2688]{1,0:T(8,128)(2,1)S(1)} collective-permute-done((bf16[384,2688]{1,0:T(8,128)(2,1)S(1)}, bf16[384,2688]{1,0:T(8,128)(2,1)S(1)}, u32[]{:S(2)}, u32[]{:S(2)}) %collective-permute-start.71) | collective-permute-done | bytes 2064416 | tf_op jit(solution)/shard_map/ppermute | solution.py:83
  887.2 44.0 %collective-permute-done.83 = bf16[384,2688]{1,0:T(8,128)(2,1)S(1)} collective-permute-done((bf16[384,2688]{1,0:T(8,128)(2,1)S(1)}, bf16[384,2688]{1,0:T(8,128)(2,1)S(1)}, u32[]{:S(2)}, u32[]{:S(2)}) %collective-permute-start.83) | collective-permute-done | bytes 2064416 | tf_op jit(solution)/shard_map/ppermute | solution.py:83
  931.4 44.0 %collective-permute-done.77 = bf16[384,2688]{1,0:T(8,128)(2,1)S(1)} collective-permute-done((bf16[384,2688]{1,0:T(8,128)(2,1)S(1)}, bf16[384,2688]{1,0:T(8,128)(2,1)S(1)}, u32[]{:S(2)}, u32[]{:S(2)}) %collective-permute-start.77) | collective-permute-done | bytes 2064416 | tf_op jit(solution)/shard_map/ppermute | solution.py:83
  981.0 80.5 %collective-permute-done.89 = bf16[384,2688]{1,0:T(8,128)(2,1)S(1)} collective-permute-done((bf16[384,2688]{1,0:T(8,128)(2,1)S(1)}, bf16[384,2688]{1,0:T(8,128)(2,1)S(1)}, u32[]{:S(2)}, u32[]{:S(2)}) %collective-permute-start.89) | collective-permute-done | bytes 2064416 | tf_op jit(solution)/shard_map/ppermute | solution.py:83
  (687 shorter events, 404.5 us)
Async XLA Ops:
  88.7 91.8 %collective-permute-start.15 = (bf16[384,2688]{1,0:T(8,128)(2,1)S(1)}, bf16[384,2688]{1,0:T(8,128)(2,1)S(1)}, u32[]{:S(2)}, u32[]{:S(2)}) collective-permute-start(bf16[384,2688]{1,0:T(8,128)(2,1)S(1)} %copy-done.5), channel_id=1, source_target_pairs={{0,8},{8,0},{16,24},{24,16},{1,9},{9,1},{17,25},{25,17},{2,10},{10... | collective-permute-start | bytes 6193160 | tf_op jit(solution)/shard_map/ppermute | solution.py:56
  119.1 61.3 %collective-permute-start.24 = (bf16[192,2688]{1,0:T(8,128)(2,1)S(1)}, bf16[192,2688]{1,0:T(8,128)(2,1)S(1)}, u32[]{:S(2)}, u32[]{:S(2)}) collective-permute-start(bf16[192,2688]{1,0:T(8,128)(2,1)S(1)} %copy-done.63), channel_id=1, source_target_pairs={{0,16},{8,24},{16,0},{24,8},{1,17},{9,25},{17,1},{25,9},{2,18},{10... | collective-permute-start | bytes 3096584 | tf_op jit(solution)/shard_map/ppermute | solution.py:39
  140.7 68.3 %collective-permute-start.23 = (bf16[384,2688]{1,0:T(8,128)(2,1)S(1)}, bf16[384,2688]{1,0:T(8,128)(2,1)S(1)}, u32[]{:S(2)}, u32[]{:S(2)}) collective-permute-start(bf16[384,2688]{1,0:T(8,128)(2,1)S(1)} %get-tuple-element.84), channel_id=1, source_target_pairs={{0,8},{8,0},{16,24},{24,16},{1,9},{9,1},{17,25},{25,17},{2,10},{10... | collective-permute-start | bytes 6193160 | tf_op jit(solution)/shard_map/ppermute | solution.py:56
  189.7 202.7 %collective-permute-start.53 = (bf16[256,768]{0,1:T(8,128)(2,1)}, bf16[256,768]{0,1:T(8,128)(2,1)}, u32[]{:S(2)}, u32[]{:S(2)}) collective-permute-start(bf16[256,768]{0,1:T(8,128)(2,1)} %bitcast.17), channel_id=1, source_target_pairs={{0,8},{8,0},{16,24},{24,16},{1,9},{9,1},{17,25},{25,17},{2,10},{10... | collective-permute-start | bytes 1179656 | tf_op jit(solution)/shard_map/ppermute | solution.py:56
  234.1 159.9 %collective-permute-start.55 = (bf16[256,768]{0,1:T(8,128)(2,1)}, bf16[256,768]{0,1:T(8,128)(2,1)}, u32[]{:S(2)}, u32[]{:S(2)}) collective-permute-start(bf16[256,768]{0,1:T(8,128)(2,1)} %collective-permute-done.54), channel_id=1, source_target_pairs={{0,8},{8,0},{16,24},{24,16},{1,9},{9,1},{17,25},{25,17},{2,10},{10... | collective-permute-start | bytes 1179656 | tf_op jit(solution)/shard_map/ppermute | solution.py:56
  392.5 55.5 %collective-permute-start.67 = (bf16[256,2688]{1,0:T(8,128)(2,1)S(1)}, bf16[256,2688]{1,0:T(8,128)(2,1)S(1)}, u32[]{:S(2)}, u32[]{:S(2)}) collective-permute-start(bf16[256,2688]{1,0:T(8,128)(2,1)S(1)} %copy-done.48), channel_id=1, source_target_pairs={{0,16},{8,24},{16,0},{24,8},{1,17},{9,25},{17,1},{25,9},{2,18},{10... | collective-permute-start | bytes 4128776 | tf_op jit(solution)/shard_map/ppermute | solution.py:51
  475.0 61.5 %collective-permute-start.63 = (bf16[256,384]{1,0:T(8,128)(2,1)S(1)}, bf16[256,384]{1,0:T(8,128)(2,1)S(1)}, u32[]{:S(2)}, u32[]{:S(2)}) collective-permute-start(bf16[256,384]{1,0:T(8,128)(2,1)S(1)} %copy-done.96), channel_id=1, source_target_pairs={{0,8},{8,0},{16,24},{24,16},{1,9},{9,1},{17,25},{25,17},{2,10},{10... | collective-permute-start | bytes 589832 | tf_op jit(solution)/shard_map/ppermute | solution.py:62
  512.9 67.0 %collective-permute-start.91 = (bf16[256,2688]{1,0:T(8,128)(2,1)}, bf16[256,2688]{1,0:T(8,128)(2,1)S(1)}, u32[]{:S(2)}, u32[]{:S(2)}) collective-permute-start(bf16[256,2688]{1,0:T(8,128)(2,1)} %pad_maximum_fusion.26), channel_id=1, source_target_pairs={{0,16},{8,24},{16,0},{24,8},{1,17},{9,25},{17,1},{25,9},{2,18},{10... | collective-permute-start | bytes 4128776 | tf_op jit(solution)/shard_map/ppermute | solution.py:51
  513.3 67.1 %collective-permute-start.85 = (bf16[256,2688]{1,0:T(8,128)(2,1)}, bf16[256,2688]{1,0:T(8,128)(2,1)S(1)}, u32[]{:S(2)}, u32[]{:S(2)}) collective-permute-start(bf16[256,2688]{1,0:T(8,128)(2,1)} %pad_maximum_fusion.25), channel_id=1, source_target_pairs={{0,16},{8,24},{16,0},{24,8},{1,17},{9,25},{17,1},{25,9},{2,18},{10... | collective-permute-start | bytes 4128776 | tf_op jit(solution)/shard_map/ppermute | solution.py:51
  523.9 56.0 %collective-permute-start.64 = (bf16[256,384]{1,0:T(8,128)(2,1)S(1)}, bf16[256,384]{1,0:T(8,128)(2,1)S(1)}, u32[]{:S(2)}, u32[]{:S(2)}) collective-permute-start(bf16[256,384]{1,0:T(8,128)(2,1)S(1)} %copy-done.94), channel_id=1, source_target_pairs={{0,16},{8,24},{16,0},{24,8},{1,17},{9,25},{17,1},{25,9},{2,18},{10... | collective-permute-start | bytes 589832 | tf_op jit(solution)/shard_map/ppermute | solution.py:62
  526.1 56.2 %collective-permute-start.65 = (bf16[256,384]{1,0:T(8,128)(2,1)S(1)}, bf16[256,384]{1,0:T(8,128)(2,1)S(1)}, u32[]{:S(2)}, u32[]{:S(2)}) collective-permute-start(bf16[256,384]{1,0:T(8,128)(2,1)S(1)} %copy-done.92), channel_id=1, source_target_pairs={{0,24},{8,16},{16,8},{24,0},{1,25},{9,17},{17,9},{25,1},{2,26},{10... | collective-permute-start | bytes 589832 | tf_op jit(solution)/shard_map/ppermute | solution.py:62
  536.5 69.9 %collective-permute-start.90 = (bf16[256,2688]{1,0:T(8,128)(2,1)}, bf16[256,2688]{1,0:T(8,128)(2,1)S(1)}, u32[]{:S(2)}, u32[]{:S(2)}) collective-permute-start(bf16[256,2688]{1,0:T(8,128)(2,1)} %pad_maximum_fusion.26), channel_id=1, source_target_pairs={{0,8},{8,0},{16,24},{24,16},{1,9},{9,1},{17,25},{25,17},{2,10},{10... | collective-permute-start | bytes 4128776 | tf_op jit(solution)/shard_map/ppermute | solution.py:56
  606.4 63.7 %collective-permute-start.69 = (bf16[384,2688]{1,0:T(8,128)(2,1)S(1)}, bf16[384,2688]{1,0:T(8,128)(2,1)S(1)}, u32[]{:S(2)}, u32[]{:S(2)}) collective-permute-start(bf16[384,2688]{1,0:T(8,128)(2,1)S(1)} %pad_maximum_fusion.16), channel_id=1, source_target_pairs={{0,2},{6,4},{1,3},{7,5},{8,10},{14,12},{9,11},{15,13},{16,18},{22,... | collective-permute-start | bytes 6193160 | tf_op jit(solution)/shard_map/ppermute | solution.py:79
  613.2 88.3 %collective-permute-start.81 = (bf16[384,2688]{1,0:T(8,128)(2,1)S(1)}, bf16[384,2688]{1,0:T(8,128)(2,1)S(1)}, u32[]{:S(2)}, u32[]{:S(2)}) collective-permute-start(bf16[384,2688]{1,0:T(8,128)(2,1)S(1)} %pad_maximum_fusion.18), channel_id=1, source_target_pairs={{0,2},{6,4},{1,3},{7,5},{8,10},{14,12},{9,11},{15,13},{16,18},{22,... | collective-permute-start | bytes 6193160 | tf_op jit(solution)/shard_map/ppermute | solution.py:79
  625.6 120.2 %collective-permute-start.75 = (bf16[384,2688]{1,0:T(8,128)(2,1)S(1)}, bf16[384,2688]{1,0:T(8,128)(2,1)S(1)}, u32[]{:S(2)}, u32[]{:S(2)}) collective-permute-start(bf16[384,2688]{1,0:T(8,128)(2,1)S(1)} %pad_maximum_fusion.17), channel_id=1, source_target_pairs={{0,2},{6,4},{1,3},{7,5},{8,10},{14,12},{9,11},{15,13},{16,18},{22,... | collective-permute-start | bytes 6193160 | tf_op jit(solution)/shard_map/ppermute | solution.py:79
  645.4 144.6 %collective-permute-start.93 = (bf16[384,2688]{1,0:T(8,128)(2,1)S(1)}, bf16[384,2688]{1,0:T(8,128)(2,1)S(1)}, u32[]{:S(2)}, u32[]{:S(2)}) collective-permute-start(bf16[384,2688]{1,0:T(8,128)(2,1)S(1)} %pad_maximum_fusion.20), channel_id=1, source_target_pairs={{0,2},{6,4},{1,3},{7,5},{8,10},{14,12},{9,11},{15,13},{16,18},{22,... | collective-permute-start | bytes 6193160 | tf_op jit(solution)/shard_map/ppermute | solution.py:79
  666.2 166.7 %collective-permute-start.87 = (bf16[384,2688]{1,0:T(8,128)(2,1)S(1)}, bf16[384,2688]{1,0:T(8,128)(2,1)S(1)}, u32[]{:S(2)}, u32[]{:S(2)}) collective-permute-start(bf16[384,2688]{1,0:T(8,128)(2,1)S(1)} %pad_maximum_fusion.19), channel_id=1, source_target_pairs={{0,2},{6,4},{1,3},{7,5},{8,10},{14,12},{9,11},{15,13},{16,18},{22,... | collective-permute-start | bytes 6193160 | tf_op jit(solution)/shard_map/ppermute | solution.py:79
  670.6 163.6 %collective-permute-start.70 = (bf16[384,2688]{1,0:T(8,128)(2,1)S(1)}, bf16[384,2688]{1,0:T(8,128)(2,1)S(1)}, u32[]{:S(2)}, u32[]{:S(2)}) collective-permute-start(bf16[384,2688]{1,0:T(8,128)(2,1)S(1)} %add_convert_fusion.9), channel_id=1, source_target_pairs={{2,4},{4,2},{3,5},{5,3},{10,12},{12,10},{11,13},{13,11},{18,20},{2... | collective-permute-start | bytes 6193160 | tf_op jit(solution)/shard_map/ppermute | solution.py:81
  702.1 134.0 %collective-permute-start.82 = (bf16[384,2688]{1,0:T(8,128)(2,1)S(1)}, bf16[384,2688]{1,0:T(8,128)(2,1)S(1)}, u32[]{:S(2)}, u32[]{:S(2)}) collective-permute-start(bf16[384,2688]{1,0:T(8,128)(2,1)S(1)} %add_convert_fusion.5), channel_id=1, source_target_pairs={{2,4},{4,2},{3,5},{5,3},{10,12},{12,10},{11,13},{13,11},{18,20},{2... | collective-permute-start | bytes 6193160 | tf_op jit(solution)/shard_map/ppermute | solution.py:81
  746.3 91.5 %collective-permute-start.76 = (bf16[384,2688]{1,0:T(8,128)(2,1)S(1)}, bf16[384,2688]{1,0:T(8,128)(2,1)S(1)}, u32[]{:S(2)}, u32[]{:S(2)}) collective-permute-start(bf16[384,2688]{1,0:T(8,128)(2,1)S(1)} %add_convert_fusion.7), channel_id=1, source_target_pairs={{2,4},{4,2},{3,5},{5,3},{10,12},{12,10},{11,13},{13,11},{18,20},{2... | collective-permute-start | bytes 6193160 | tf_op jit(solution)/shard_map/ppermute | solution.py:81
  836.5 94.6 %collective-permute-start.83 = (bf16[384,2688]{1,0:T(8,128)(2,1)S(1)}, bf16[384,2688]{1,0:T(8,128)(2,1)S(1)}, u32[]{:S(2)}, u32[]{:S(2)}) collective-permute-start(bf16[384,2688]{1,0:T(8,128)(2,1)S(1)} %add_convert_fusion.4), channel_id=1, source_target_pairs={{2,0},{4,6},{3,1},{5,7},{10,8},{12,14},{11,9},{13,15},{18,16},{20,... | collective-permute-start | bytes 6193160 | tf_op jit(solution)/shard_map/ppermute | solution.py:83
  838.3 137.0 %collective-permute-start.77 = (bf16[384,2688]{1,0:T(8,128)(2,1)S(1)}, bf16[384,2688]{1,0:T(8,128)(2,1)S(1)}, u32[]{:S(2)}, u32[]{:S(2)}) collective-permute-start(bf16[384,2688]{1,0:T(8,128)(2,1)S(1)} %add_convert_fusion.6), channel_id=1, source_target_pairs={{2,0},{4,6},{3,1},{5,7},{10,8},{12,14},{11,9},{13,15},{18,16},{20,... | collective-permute-start | bytes 6193160 | tf_op jit(solution)/shard_map/ppermute | solution.py:83
  840.1 223.6 %collective-permute-start.95 = (bf16[384,2688]{1,0:T(8,128)(2,1)S(1)}, bf16[384,2688]{1,0:T(8,128)(2,1)S(1)}, u32[]{:S(2)}, u32[]{:S(2)}) collective-permute-start(bf16[384,2688]{1,0:T(8,128)(2,1)S(1)} %add_convert_fusion), channel_id=1, source_target_pairs={{2,0},{4,6},{3,1},{5,7},{10,8},{12,14},{11,9},{13,15},{18,16},{20,... | collective-permute-start | bytes 6193160 | tf_op jit(solution)/shard_map/ppermute | solution.py:83
  841.9 219.6 %collective-permute-start.89 = (bf16[384,2688]{1,0:T(8,128)(2,1)S(1)}, bf16[384,2688]{1,0:T(8,128)(2,1)S(1)}, u32[]{:S(2)}, u32[]{:S(2)}) collective-permute-start(bf16[384,2688]{1,0:T(8,128)(2,1)S(1)} %add_convert_fusion.2), channel_id=1, source_target_pairs={{2,0},{4,6},{3,1},{5,7},{10,8},{12,14},{11,9},{13,15},{18,16},{20,... | collective-permute-start | bytes 6193160 | tf_op jit(solution)/shard_map/ppermute | solution.py:83
  (215 other events, 3295.1 us)

commit v2 on v1

v2 whole, which is shorter than its diff:
```python
import math

import jax
import jax.numpy as jnp
from jax import lax
from jax.experimental import pallas as pl
from jax.experimental.pallas import tpu as pltpu
from jax.sharding import PartitionSpec as P

HEAD_DIM = 128


EPSILON = 1e-06
ROPE_BASE = 1000000.0


def xor_pairs(size, mask):
    return [(i, i ^ mask) for i in range(size)]


class Lane:
    def __init__(self, depth=1):
        self.sent = []
        self.depth = depth

    def send(self, array, axis, pairs):
        if len(self.sent) >= self.depth:
            array, _ = lax.optimization_barrier((array, self.sent[-self.depth]))
        got = lax.ppermute(array, axis, pairs)
        self.sent.append(got)
        return got


def far_masks(size):
    masks, mask = [], 2
    while mask < size:
        masks.append(mask)
        mask *= 2
    return masks


def swap_blocks(blocks, me):
    mask = 1
    while mask < len(blocks):
        flag = (me & mask) != 0
        blocks = [jnp.where(flag, blocks[r ^ mask], blocks[r]) for r in range(len(blocks))]
        mask *= 2
    return blocks


def far_half(piece, mask, size, parity, lanes):
    half = piece.shape[0] // 2
    sent = lax.dynamic_slice_in_dim(piece, half * parity, half, 0)
    straight = lanes["x"].send(sent, "dp", xor_pairs(size, mask))
    other = lanes["z"].send(straight, "context", xor_pairs(lax.axis_size("context"), 1))
    first = jnp.where(parity == 0, straight, other)
    second = jnp.where(parity == 0, other, straight)
    return jnp.concatenate([first, second], 0)


def far_pieces(own, size, lanes, parity=None):
    pieces = {0: own}
    for mask in far_masks(size):
        for r in list(pieces):
            if parity is None:
                pieces[r ^ mask] = lanes["x"].send(pieces[r], "dp", xor_pairs(size, mask))
            else:
                pieces[r ^ mask] = far_half(pieces[r], mask, size, parity, lanes)
    return pieces


def gather_pieces(own, size, lanes, parity=None):
    pieces = far_pieces(own, size, lanes, parity)
    for r in list(pieces):
        pieces[r ^ 1] = lax.ppermute(pieces[r], "dp", xor_pairs(size, 1))
    return [pieces[r] for r in range(size)]


def trade_blocks(blocks, size):
    return [blocks[0]] + [
        lax.ppermute(blocks[r], "dp", xor_pairs(size, r)) for r in range(1, size)
    ]


def tensor_sum(part):
    sent = part.astype(jnp.bfloat16)
    size = lax.axis_size("tensor")
    if size == 2:
        other = lax.ppermute(sent, "tensor", [(0, 1), (1, 0)])
        return sent.astype(jnp.float32) + other.astype(jnp.float32)
    return lax.psum(part, "tensor")


def line_sum(part, lanes):
    place = lax.axis_index("context")
    if lax.axis_size("context") != 4:
        return lax.psum(part.astype(jnp.float32), "context")
    got = lanes["hop1"].send(part, "context", [(0, 1), (3, 2)])
    pair = (part.astype(jnp.float32) + got.astype(jnp.float32)).astype(jnp.bfloat16)
    got = lanes["hop2"].send(pair, "context", [(1, 2), (2, 1)])
    total = (pair.astype(jnp.float32) + got.astype(jnp.float32)).astype(jnp.bfloat16)
    got = lanes["hop3"].send(total, "context", [(1, 0), (2, 3)])
    ends = (place == 0) | (place == 3)
    return jnp.where(ends, got, total).astype(jnp.float32)


def small_total(vector):
    for axis in ("dp", "context"):
        size, mask = lax.axis_size(axis), 1
        while mask < size:
            vector = vector + lax.ppermute(vector, axis, xor_pairs(size, mask))
            mask *= 2
    return vector


def contract_last(left, right):
    return lax.dot_general(
        left, right, (((1,), (1,)), ((), ())), preferred_element_type=jnp.float32
    )


def norm_back(field, scale_rows, gain, d_normed):
    weighted = d_normed * gain
    cubed = scale_rows * scale_rows * scale_rows
    return scale_rows * weighted - field * cubed * jnp.mean(field * weighted, -1, keepdims=True)


ANY = pl.BlockSpec(memory_space=pl.ANY)
VMEM = pl.BlockSpec(memory_space=pltpu.VMEM)
SMEM = pl.BlockSpec(memory_space=pltpu.SMEM)


def plain_params(limit):
    return pltpu.CompilerParams(vmem_limit_bytes=limit)


def dot_nn(left, right):
    return jnp.dot(left, right, preferred_element_type=jnp.float32)


def feed_chunk(two_row, fall_row, sources, start, width, d_sum, out_sum):
    rows, features = two_row.shape
    bf16, f32 = jnp.bfloat16, jnp.float32
    flat, layout = [], []
    for source in sources:
        layout.append(len(source))
        flat.extend(source)
    first = d_sum is None
    held = [] if first else [d_sum, out_sum]

    def kernel(*refs):
        refs = list(refs)
        two_ref, fall_ref = refs[:2]
        given = refs[2 : 2 + len(flat)]
        at = 2 + len(flat)
        sums = refs[at : at + len(held)]
        at += len(held)
        acts_ref, d_ref, out_ref, gate_w, up_w, down_w, sems = refs[at:]
        copies = [[], [], []]
        place, taken = 0, 0
        for kind in layout:
            depth = given[taken].shape[0]
            for which, scratch in enumerate((gate_w, up_w, down_w)):
                if kind == 3:
                    view = given[taken + which].at[:, pl.ds(start, width)]
                else:
                    view = given[taken].at[:, pl.ds(which * width, width)]
                copy = pltpu.make_async_copy(
                    view,
                    scratch.at[pl.ds(place, depth), :],
                    sems.at[which, len(copies[which])],
                )
                copies[which].append(copy)
            place += depth
            taken += kind
        for group in copies:
            for copy in group:
                copy.start()
        for copy in copies[0]:
            copy.wait()
        gate = dot_nn(two_ref[...], gate_w[...])
        for copy in copies[1]:
            copy.wait()
        up = dot_nn(two_ref[...], up_w[...])
        for copy in copies[2]:
            copy.wait()
        d_active = dot_nn(fall_ref[...], down_w[...])
        sigmoid = jax.nn.sigmoid(gate)
        swish = gate * sigmoid
        acts_ref[:, 2 * width :] = (swish * up).astype(bf16)
        acts_ref[:, :width] = (d_active * up * sigmoid * (1.0 + gate * (1.0 - sigmoid))).astype(bf16)
        acts_ref[:, width : 2 * width] = (d_active * swish).astype(bf16)
        d_part = contract_last(acts_ref[:, :width], gate_w[...]) + contract_last(
            acts_ref[:, width : 2 * width], up_w[...]
        )
        out_part = contract_last(acts_ref[:, 2 * width :], down_w[...])
        if first:
            d_ref[...] = d_part
            out_ref[...] = out_part
        else:
            d_ref[...] = sums[0][...] + d_part
            out_ref[...] = sums[1][...] + out_part

    weight_bytes = 6 * features * width
    return pl.pallas_call(
        kernel,
        out_shape=(
            jax.ShapeDtypeStruct((rows, 3 * width), bf16),
            jax.ShapeDtypeStruct((rows, features), f32),
            jax.ShapeDtypeStruct((rows, features), f32),
        ),
        in_specs=[VMEM, VMEM] + [ANY] * len(flat) + [VMEM] * len(held),
        out_specs=(VMEM, VMEM, VMEM),
        scratch_shapes=[pltpu.VMEM((features, width), bf16)] * 3
        + [pltpu.SemaphoreType.DMA((3, len(sources)))],
        compiler_params=plain_params(40 << 20),
        cost_estimate=pl.CostEstimate(
            flops=12 * rows * features * width,
            bytes_accessed=weight_bytes + 20 * rows * features + 6 * rows * width,
            transcendentals=rows * width,
        ),
        name="feed_chunk",
    )(two_row, fall_row, *flat, *held)


def grad_block(features, pieces, spans):
    bf16 = jnp.bfloat16
    depth, columns = pieces[0].shape
    tokens = features[0].shape[1]
    own = features[0].shape[0]
    total = sum(w for _, w in spans)

    def kernel(*refs):
        refs = list(refs)
        feature_refs = refs[: len(features)]
        given = refs[len(features) : len(features) + len(pieces)]
        out_ref, held, sems = refs[len(features) + len(pieces) :]
        copies = [
            pltpu.make_async_copy(ref, held.at[pl.ds(n * depth, depth), :], sems.at[n])
            for n, ref in enumerate(given)
        ]
        for copy in copies:
            copy.start()
        for copy in copies:
            copy.wait()
        for ref, (start, width) in zip(feature_refs, spans):
            out_ref[:, start : start + width] = dot_nn(
                ref[...], held[:, start : start + width]
            ).astype(bf16)

    return pl.pallas_call(
        kernel,
        out_shape=jax.ShapeDtypeStruct((own, total), bf16),
        in_specs=[VMEM] * len(features) + [ANY] * len(pieces),
        out_specs=VMEM,
        scratch_shapes=[
            pltpu.VMEM((tokens, columns), bf16),
            pltpu.SemaphoreType.DMA((len(pieces),)),
        ],
        compiler_params=plain_params(40 << 20),
        cost_estimate=pl.CostEstimate(
            flops=2 * own * tokens * total,
            bytes_accessed=2 * (tokens * columns + own * total + own * tokens),
            transcendentals=0,
        ),
        name="grad_block",
    )(*features, *pieces)


def key_bias_table(place, length, keys, block_len):
    key_at = lax.broadcasted_iota(jnp.int32, (keys, block_len), 0)
    query_at = lax.broadcasted_iota(jnp.int32, (keys, block_len), 1) + place * block_len
    shift = key_at // block_len
    key_at = key_at - shift * block_len + (place - shift) * block_len
    seen = (key_at <= query_at) & (key_at < length) & (key_at >= 0)
    return jnp.where(seen, 0.0, -1e30).astype(jnp.float32)


def attend(facts, query, pair):
    rows, width = query.shape
    keys = pair.shape[0]
    heads = width // HEAD_DIM
    bf16, f32 = jnp.bfloat16, jnp.float32
    scale = 1.0 / math.sqrt(HEAD_DIM)

    def kernel(facts_ref, query_ref, pair_ref, mixed_ref, lse_ref, bias, value_t):
        bias[...] = key_bias_table(facts_ref[0], facts_ref[1], keys, rows)
        value_t[...] = pair_ref[:, HEAD_DIM:].T
        lse_ref[...] = jnp.zeros_like(lse_ref)
        for head in range(heads):
            cols = slice(head * HEAD_DIM, (head + 1) * HEAD_DIM)
            scores = contract_last(pair_ref[:, :HEAD_DIM], query_ref[:, cols]) * scale + bias[...]
            top = jnp.max(scores, 0, keepdims=True)
            raised = jnp.exp(scores - top)
            total = jnp.sum(raised, 0, keepdims=True)
            lse_ref[head : head + 1, :] = top + jnp.log(total)
            probs = (raised * (1.0 / total)).astype(bf16)
            mixed_ref[:, cols] = dot_nn(value_t[...], probs).T.astype(bf16)

    return pl.pallas_call(
        kernel,
        out_shape=(
            jax.ShapeDtypeStruct((rows, width), bf16),
            jax.ShapeDtypeStruct((8, rows), f32),
        ),
        in_specs=[SMEM, VMEM, VMEM],
        out_specs=(VMEM, VMEM),
        scratch_shapes=[pltpu.VMEM((keys, rows), f32), pltpu.VMEM((HEAD_DIM, keys), bf16)],
        compiler_params=plain_params(40 << 20),
        cost_estimate=pl.CostEstimate(
            flops=4 * rows * keys * width + 12 * heads * rows * keys * 100,
            bytes_accessed=4 * rows * width + 4 * keys * HEAD_DIM,
            transcendentals=heads * rows * keys,
        ),
        name="attend",
    )(facts, query, pair)


def turn(field, cosine, sine):
    return field * cosine + pltpu.roll(field, HEAD_DIM // 2, 1) * sine


def attend_back(facts, query, pair, lse, d_mixed, cosine, sine):
    rows, width = query.shape
    keys = pair.shape[0]
    heads = width // HEAD_DIM
    bf16, f32 = jnp.bfloat16, jnp.float32
    scale = 1.0 / math.sqrt(HEAD_DIM)

    def kernel(facts_ref, query_ref, pair_ref, lse_ref, d_mixed_ref, cos_ref, sin_ref, d_query_ref, d_own_ref, d_rest_ref, bias, key_t, d_key, d_value):
        bias[...] = key_bias_table(facts_ref[0], facts_ref[1], keys, rows)
        key_t[...] = pair_ref[:, :HEAD_DIM].T
        for head in range(heads):
            cols = slice(head * HEAD_DIM, (head + 1) * HEAD_DIM)
            scores = contract_last(pair_ref[:, :HEAD_DIM], query_ref[:, cols]) * scale + bias[...]
            probs = jnp.exp(scores - lse_ref[head : head + 1, :])
            d_probs = contract_last(pair_ref[:, HEAD_DIM:], d_mixed_ref[:, cols])
            inner = jnp.sum(d_probs * probs, 0, keepdims=True)
            d_scores = (probs * (d_probs - inner)).astype(bf16)
            d_query = (dot_nn(key_t[...], d_scores) * scale).T
            d_query_ref[:, cols] = turn(d_query, cos_ref[...], -sin_ref[...]).astype(bf16)
            more_key = dot_nn(d_scores, query_ref[:, cols])
            more_value = dot_nn(probs.astype(bf16), d_mixed_ref[:, cols])
            if head == 0:
                d_key[...] = more_key
                d_value[...] = more_value
            else:
                d_key[...] += more_key
                d_value[...] += more_value
        d_own_ref[:, :HEAD_DIM] = d_key[:rows, :] * scale
        d_own_ref[:, HEAD_DIM:] = d_value[:rows, :]
        d_rest_ref[:, :HEAD_DIM] = (d_key[rows:, :] * scale).astype(bf16)
        d_rest_ref[:, HEAD_DIM:] = d_value[rows:, :].astype(bf16)

    return pl.pallas_call(
        kernel,
        out_shape=(
            jax.ShapeDtypeStruct((rows, width), bf16),
            jax.ShapeDtypeStruct((rows, 2 * HEAD_DIM), f32),
            jax.ShapeDtypeStruct((keys - rows, 2 * HEAD_DIM), bf16),
        ),
        in_specs=[SMEM] + [VMEM] * 6,
        out_specs=(VMEM, VMEM, VMEM),
        scratch_shapes=[
            pltpu.VMEM((keys, rows), f32),
            pltpu.VMEM((HEAD_DIM, keys), bf16),
            pltpu.VMEM((keys, HEAD_DIM), f32),
            pltpu.VMEM((keys, HEAD_DIM), f32),
        ],
        compiler_params=plain_params(40 << 20),
        cost_estimate=pl.CostEstimate(
            flops=10 * rows * keys * width + 12 * heads * rows * keys * 200,
            bytes_accessed=8 * rows * width + 8 * keys * HEAD_DIM,
            transcendentals=heads * rows * keys,
        ),
        name="attend_back",
    )(facts, query, pair, lse, d_mixed, cosine, sine)


MESH = pl.DeviceIdType.MESH


def flipped(index, mask):
    return index + mask - 2 * mask * ((index // mask) % 2)


def gather_and_sum(units, features, blocks, size):
    bf16, f32 = jnp.bfloat16, jnp.float32
    count = len(units)
    gathered = [isinstance(u, (list, tuple)) for u in units]
    flat = [a for u in units for a in (u if isinstance(u, (list, tuple)) else [u])]
    starts, at = [], 0
    for u in units:
        starts.append(at)
        at += len(u) if isinstance(u, (list, tuple)) else 1
    rows = flat[0].shape[0]
    widest = max(a.shape[1] for a in flat)
    own_rows, tokens = features[0].shape
    widths = []
    where = []
    counts = {}
    for u, group in enumerate(blocks):
        for spans in group:
            width = sum(w for _, _, w in spans)
            if width not in counts:
                counts[width] = 0
                widths.append(width)
            where.append((u, spans, widths.index(width), counts[width]))
            counts[width] += 1
    block_count = len(where)
    steps = []
    held = [0]
    for mask in far_masks(size):
        for r in list(held):
            steps.append((r, mask))
            held.append(r ^ mask)
    for r in list(held):
        steps.append((r, 1))
    arrival = {r ^ mask: n for n, (r, mask) in enumerate(steps)}
    ahead = 2

    def kernel(*refs):
        refs = list(refs)
        unit_refs, refs = refs[: len(flat)], refs[len(flat) :]
        feature_refs, refs = refs[: len(features)], refs[len(features) :]
        outs, refs = refs[: len(widths)], refs[len(widths) :]
        land, refs = refs[0], refs[1:]
        mine, refs = refs[: len(widths)], refs[len(widths) :]
        first, refs = refs[: len(widths)], refs[len(widths) :]
        second, refs = refs[: len(widths)], refs[len(widths) :]
        table, send_g, recv_g, send_a, recv_a, send_b, recv_b, load, store = refs
        me = lax.axis_index("dp")
        place = lax.axis_index("context")
        middle = place * (3 - place) == 2
        inner = 1 + place // 2
        across = 3 - place
        outer = 3 * (place - 1)

        barrier = pltpu.get_barrier_semaphore()
        partners = sorted(set(mask for _, mask in steps))
        for mask in partners:
            pl.semaphore_signal(barrier, 1, device_id={"dp": flipped(me, mask)}, device_id_type=MESH)

        @pl.when(middle)
        def _():
            pl.semaphore_signal(barrier, 1, device_id={"context": across}, device_id_type=MESH)
            pl.semaphore_signal(barrier, 1, device_id={"context": outer}, device_id_type=MESH)
            pl.semaphore_wait(barrier, len(partners) + 2)

        @pl.when(jnp.logical_not(middle))
        def _():
            pl.semaphore_signal(barrier, 1, device_id={"context": inner}, device_id_type=MESH)
            pl.semaphore_wait(barrier, len(partners) + 1)

        def piece(u, r):
            if gathered[u]:
                return unit_refs[starts[u] + r]
            if r == 0:
                return unit_refs[starts[u]]
            return land.at[r - 1, u, :, pl.ds(0, flat[starts[u]].shape[1])]

        def transfer(u, n):
            r, mask = steps[n]
            target = r ^ mask
            return pltpu.make_async_remote_copy(
                src_ref=piece(u, r),
                dst_ref=land.at[target - 1, u, :, pl.ds(0, flat[starts[u]].shape[1])],
                send_sem=send_g.at[n, u],
                recv_sem=recv_g.at[n, u],
                device_id={"dp": flipped(me, mask)},
                device_id_type=MESH,
            )

        wanted = [u for u in range(count) if not gathered[u]]

        def begin(u):
            for n, (r, _) in enumerate(steps):
                if r == 0:
                    transfer(u, n).start()

        def loads(u, slot):
            width = flat[starts[u]].shape[1]
            return [
                pltpu.make_async_copy(
                    piece(u, r),
                    table.at[slot, pl.ds(r * rows, rows), pl.ds(0, width)],
                    load.at[slot, r],
                )
                for r in range(size)
            ]

        def forward(u):
            waited = set()
            for n, (r, mask) in enumerate(steps):
                if r != 0:
                    if r not in waited:
                        transfer(u, arrival[r]).wait_recv()
                        waited.add(r)
                    transfer(u, n).start()
            for r in range(1, size):
                if r not in waited:
                    transfer(u, arrival[r]).wait_recv()

        def hop(j, source, target, place_to, send, recv):
            _, _, kind, index = where[j]
            return pltpu.make_async_remote_copy(
                src_ref=source[kind].at[index],
                dst_ref=target[kind].at[index],
                send_sem=send.at[j],
                recv_sem=recv.at[j],
                device_id={"context": place_to},
                device_id_type=MESH,
            )

        def hop_in(j):
            return hop(j, mine, first, inner, send_a, recv_a)

        def hop_across(j):
            return hop(j, mine, second, across, send_b, recv_b)

        def hop_out(j):
            return hop(j, first, first, outer, send_a, recv_a)

        def keep(j):
            _, _, kind, index = where[j]
            return pltpu.make_async_copy(first[kind].at[index], outs[kind].at[index], store.at[j])

        def total_in(j):
            _, _, kind, index = where[j]
            hop_in(j).wait_recv()
            mine[kind][index] = (
                mine[kind][index].astype(f32) + first[kind][index].astype(f32)
            ).astype(bf16)
            hop_across(j).start()

        def total_across(j):
            _, _, kind, index = where[j]
            hop_across(j).wait_recv()
            first[kind][index] = (
                mine[kind][index].astype(f32) + second[kind][index].astype(f32)
            ).astype(bf16)
            hop_out(j).start()
            keep(j).start()

        of_unit = [[j for j in range(block_count) if where[j][0] == u] for u in range(count)]
        for u in wanted[:ahead]:
            begin(u)
        for copy in loads(0, 0) if gathered[0] else []:
            copy.start()
        middle_in = []
        for u in range(count):
            slot = u % 2
            if not gathered[u]:
                forward(u)
                later = [v for v in wanted if v > u]
                if len(later) >= ahead:
                    begin(later[ahead - 1])
            if not (u == 0 and gathered[0]):
                for copy in loads(u, slot):
                    copy.start()
            for copy in loads(u, slot):
                copy.wait()
            for j in of_unit[u]:
                _, spans, kind, index = where[j]
                filled = 0
                for which, start, width in spans:
                    mine[kind][index, :, filled : filled + width] = dot_nn(
                        feature_refs[which][...], table[slot, :, start : start + width]
                    ).astype(bf16)
                    filled += width

                @pl.when(jnp.logical_not(middle))
                def _(j=j):
                    if j >= 3:
                        hop_in(j - 3).wait_send()
                    hop_in(j).start()

            if u >= 1:

                @pl.when(middle)
                def _(u=u):
                    for j in of_unit[u - 1]:
                        total_in(j)
                        if j >= 1:
                            total_across(j - 1)

        @pl.when(middle)
        def _():
            for j in of_unit[count - 1]:
                total_in(j)
                total_across(j - 1)
            total_across(block_count - 1)
            for j in range(block_count):
                hop_across(j).wait_send()
                hop_out(j).wait_send()
                keep(j).wait()

        @pl.when(jnp.logical_not(middle))
        def _():
            for j in range(max(block_count - 3, 0), block_count):
                hop_in(j).wait_send()
            for j in range(block_count):
                hop_out(j).wait_recv()
                keep(j).start()
            for j in range(block_count):
                keep(j).wait()

        for u in wanted:
            for n in range(len(steps)):
                transfer(u, n).wait_send()

    def stacks(kind_memory):
        return [kind_memory((counts[w], own_rows, w), bf16) for w in widths]

    columns = sum(counts[w] * w for w in widths)
    results = pl.pallas_call(
        kernel,
        out_shape=[jax.ShapeDtypeStruct((counts[w], own_rows, w), bf16) for w in widths]
        + [jax.ShapeDtypeStruct((size - 1, count, rows, widest), bf16)],
        in_specs=[ANY] * len(flat) + [VMEM] * len(features),
        out_specs=[ANY] * (len(widths) + 1),
        scratch_shapes=stacks(pltpu.VMEM) * 3
        + [
            pltpu.VMEM((2, tokens, widest), bf16),
            pltpu.SemaphoreType.DMA((len(steps), count)),
            pltpu.SemaphoreType.DMA((len(steps), count)),
            pltpu.SemaphoreType.DMA((block_count,)),
            pltpu.SemaphoreType.DMA((block_count,)),
            pltpu.SemaphoreType.DMA((block_count,)),
            pltpu.SemaphoreType.DMA((block_count,)),
            pltpu.SemaphoreType.DMA((2, size)),
            pltpu.SemaphoreType.DMA((block_count,)),
        ],
        compiler_params=pltpu.CompilerParams(
            collective_id=0, has_side_effects=True, vmem_limit_bytes=60 << 20
        ),
        cost_estimate=pl.CostEstimate(
            flops=2 * own_rows * tokens * columns,
            bytes_accessed=2 * tokens * columns + 12 * own_rows * columns,
            transcendentals=0,
        ),
        name="gather_and_sum",
    )(*flat, *features)
    return [(results[kind], index) for _, _, kind, index in where]


def chunk_edges(columns):
    tiles = columns // 128
    count = next((n for n in (7, 5, 4, 6, 3, 2) if tiles % n == 0), 1)
    width = columns // count
    return [(n * width, width) for n in range(count)]


def local(
    tokens,
    lengths,
    gain_one,
    w_query,
    b_query,
    key_weight,
    key_bias,
    value_weight,
    value_bias,
    w_out,
    gain_two,
    w_gate,
    w_up,
    w_down,
    grad_out,
):
    bf16, f32 = jnp.bfloat16, jnp.float32
    seq_count, block_len, model_width = tokens.shape
    row_count = seq_count * block_len
    query_cols = w_query.shape[1]
    key_cols = key_weight.shape[1]
    unit_cols = w_gate.shape[1]
    own_rows = w_query.shape[0]
    head_count = query_cols // HEAD_DIM
    kv_count = key_cols // HEAD_DIM
    query_group_width = head_count // kv_count
    size = lax.axis_size("dp")
    me = lax.axis_index("dp")
    blocks_along = lax.axis_size("context")
    place = lax.axis_index("context")
    parity = place % 2 if blocks_along % 2 == 0 and own_rows % 32 == 0 else None

    def relative(field):
        return swap_blocks([field[:, n * own_rows : (n + 1) * own_rows] for n in range(size)], me)

    def absolute(blocks):
        return jnp.concatenate(swap_blocks(blocks, me), 1)

    def dot_rows(blocks, weights):
        return jnp.dot(
            jnp.concatenate(blocks, 1), jnp.concatenate(weights, 0), preferred_element_type=f32
        )

    lanes = {name: Lane() for name in ("x", "z", "hop1", "hop2", "hop3")}
    attention_weights = gather_pieces(
        jnp.concatenate([w_query, key_weight, value_weight], 1), size, lanes
    )
    out_weights = gather_pieces(w_out, size, lanes, parity)
    edges = chunk_edges(unit_cols)
    feed_weights = []
    early = len(edges) - 2

    feed_own = (w_gate, w_up, w_down)
    feed_near = tuple(lax.ppermute(w, "dp", xor_pairs(size, 1)) for w in feed_own)

    def fetch(start, width):
        own = jnp.concatenate([w[:, start : start + width] for w in feed_own], 1)
        far = far_pieces(own, size, lanes, parity)
        sources = []
        for r in range(size):
            if r < 2:
                sources.append(feed_own if r == 0 else feed_near)
            elif r % 2 == 0:
                sources.append((far[r],))
            else:
                sources.append((lax.ppermute(far[r - 1], "dp", xor_pairs(size, 1)),))
        feed_weights.append(sources)

    for start, width in edges[:early]:
        fetch(start, width)

    positions = place * block_len + jnp.arange(block_len, dtype=jnp.int32)
    position_count = block_len * blocks_along
    valid_rows = (positions[None, :] < lengths[:, None]).astype(f32).reshape(row_count, 1)
    facts = jnp.stack([place.astype(jnp.int32), lengths[0]])
    half = HEAD_DIM // 2
    inverse = jnp.exp(jnp.arange(half, dtype=f32) * (-2.0 * math.log(ROPE_BASE) / HEAD_DIM))
    angles = positions.astype(f32)[:, None] * inverse[None, :]
    cosine = jnp.concatenate([jnp.cos(angles)] * 2, 1)
    sine = jnp.concatenate([-jnp.sin(angles), jnp.sin(angles)], 1)
    gain_first = gain_one.astype(f32)
    gain_second = gain_two.astype(f32)
    inputs = tokens.reshape(row_count, model_width).astype(f32)
    scale_one = lax.rsqrt(jnp.mean(inputs * inputs, -1, keepdims=True) + EPSILON)
    normalized_input = (inputs * scale_one * gain_first).astype(bf16)
    normed_blocks = relative(normalized_input)
    projected = dot_rows(normed_blocks, attention_weights) + jnp.concatenate(
        [b_query, key_bias, value_bias]
    ).astype(f32)
    turned = query_cols + key_cols

    def turn_heads(field, sine_rows):
        grid = field.reshape(row_count, field.shape[1] // HEAD_DIM, HEAD_DIM)
        swapped = jnp.concatenate([grid[..., half:], grid[..., :half]], -1)
        grid = grid * cosine[:, None, :] + swapped * sine_rows[:, None, :]
        return grid.reshape(field.shape).astype(bf16)

    turned_rows = turn_heads(projected[:, :turned], sine)
    query_rot = turned_rows[:, :query_cols]
    pair_rows = jnp.concatenate([turned_rows[:, query_cols:], projected[:, turned:].astype(bf16)], 1)
    pair_all = [pair_rows]
    for shift in range(1, blocks_along):
        pair_all.append(
            lax.ppermute(
                pair_rows, "context", [(n, n + shift) for n in range(blocks_along - shift)]
            )
        )
    pair_all = jnp.concatenate(pair_all, 0)
    mixed_heads, lse = attend(facts, query_rot, pair_all)
    full_out = jnp.concatenate(out_weights, 0)
    branch = contract_last(mixed_heads, full_out)
    branch = absolute([branch[:, r * own_rows : (r + 1) * own_rows] for r in range(size)])
    hidden = inputs + tensor_sum(branch)
    scale_two = lax.rsqrt(jnp.mean(hidden * hidden, -1, keepdims=True) + EPSILON)
    normed_two = (hidden * scale_two * gain_second).astype(bf16)
    fall_grad = grad_out.reshape(row_count, model_width).astype(f32) * valid_rows
    fall_low = fall_grad.astype(bf16)
    fall_blocks = relative(fall_low)
    two_blocks = relative(normed_two)
    traded_early = trade_blocks(
        [jnp.concatenate([a, b], 1) for a, b in zip(normed_blocks, fall_blocks)], size
    )
    traded_early = jnp.concatenate(traded_early, 0).T
    normed_features, fall_features = traded_early[:own_rows], traded_early[own_rows:]
    two_features = jnp.concatenate(trade_blocks(two_blocks, size), 0).T
    two_row = jnp.concatenate(two_blocks, 1)
    fall_row = jnp.concatenate(fall_blocks, 1)

    feed_out, d_normed_two = None, None
    feed_units = []
    for turn_at, (start, width) in enumerate(edges):
        acts, d_normed_two, feed_out = feed_chunk(
            two_row, fall_row, feed_weights[turn_at], start, width, d_normed_two, feed_out
        )
        if turn_at < 0:
            acts = gather_pieces(acts, size, lanes)
        feed_units.append(acts)
        if turn_at == 0:
            for edge in edges[early:]:
                fetch(*edge)

    def split(field):
        return [field[:, r * own_rows : (r + 1) * own_rows] for r in range(size)]

    d_normed_two = tensor_sum(absolute(split(d_normed_two)))
    result = valid_rows * (hidden + tensor_sum(absolute(split(feed_out))))
    output = result.astype(bf16).reshape(seq_count, block_len, model_width)
    gain_two_grad = jnp.sum(d_normed_two * hidden * scale_two, 0)
    d_hidden = fall_grad + norm_back(hidden, scale_two, gain_second, d_normed_two)
    d_branch = d_hidden.astype(bf16)
    branch_blocks = relative(d_branch)
    branch_features = jnp.concatenate(trade_blocks(branch_blocks, size), 0).T
    d_mixed = jnp.dot(
        jnp.concatenate(branch_blocks, 1), full_out, preferred_element_type=f32
    ).astype(bf16)
    d_query_low, d_own, d_rest = attend_back(
        facts, query_rot, pair_all, lse, d_mixed, cosine, sine
    )
    for shift in range(1, blocks_along):
        d_own = d_own + lax.ppermute(
            d_rest[(shift - 1) * block_len : shift * block_len],
            "context",
            [(n, n - shift) for n in range(shift, blocks_along)],
        ).astype(f32)
    d_key_low = turn_heads(d_own[:, :key_cols], -sine)
    d_value_low = d_own[:, key_cols:].astype(bf16)
    d_projected = jnp.concatenate([d_query_low, d_key_low, d_value_low], 1)
    d_normed = contract_last(d_projected, jnp.concatenate(attention_weights, 0))
    d_normed = tensor_sum(absolute(split(d_normed)))
    gain_one_grad = jnp.sum(d_normed * inputs * scale_one, 0)
    d_inputs = d_hidden + norm_back(inputs, scale_one, gain_first, d_normed)
    grad_tokens = d_inputs.astype(bf16).reshape(seq_count, block_len, model_width)
    gain_two_grad = small_total(gain_two_grad)
    small = small_total(
        jnp.concatenate([gain_one_grad, jnp.sum(d_projected.astype(f32), 0)])
    )
    projected_width = d_projected.shape[1]
    last = jnp.concatenate([d_projected, mixed_heads], 1)
    halfway = last.shape[1] // 2
    blocks = [
        [[(0, 0, width)], [(0, width, width)], [(1, 2 * width, width)]] for _, width in edges
    ] + [
        [
            [(2, 0, halfway)],
            [(2, halfway, projected_width - halfway), (3, projected_width, query_cols)],
        ]
    ]
    sums = gather_and_sum(
        feed_units + [last],
        [two_features, fall_features, normed_features, branch_features],
        blocks,
        size,
    )

    def columns(which):
        stack = sums[which][0]
        return jnp.concatenate(
            [stack[3 * n + which].astype(f32) for n in range(len(edges))], 1
        )

    stack = sums[-1][0]
    last_grad = jnp.concatenate([stack[0], stack[1]], 1).astype(f32)
    projected_grad, out_grad = last_grad[:, :projected_width], last_grad[:, projected_width:]

    low, high = model_width + query_cols, model_width + query_cols + key_cols
    return (
        output,
        grad_tokens,
        small[:model_width],
        projected_grad[:, :query_cols],
        small[model_width:low],
        projected_grad[:, query_cols : query_cols + key_cols],
        small[low:high],
        projected_grad[:, query_cols + key_cols :],
        small[high:],
        out_grad,
        gain_two_grad,
        columns(0),
        columns(1),
        columns(2),
    )


def solution(mesh):
    in_specs = (
        P("dp", "context", None),
        P("dp"),
        P(),
        P("dp", "tensor"),
        P("tensor"),
        P("dp", "tensor"),
        P("tensor"),
        P("dp", "tensor"),
        P("tensor"),
        P("dp", "tensor"),
        P(),
        P("dp", "tensor"),
        P("dp", "tensor"),
        P("dp", "tensor"),
        P("dp", "context", None),
    )
    out_specs = (
        P("dp", "context", None),
        P("dp", "context", None),
        P(),
        P("dp", "tensor"),
        P("tensor"),
        P("dp", "tensor"),
        P("tensor"),
        P("dp", "tensor"),
        P("tensor"),
        P("dp", "tensor"),
        P(),
        P("dp", "tensor"),
        P("dp", "tensor"),
        P("dp", "tensor"),
    )
    return jax.shard_map(local, mesh=mesh, in_specs=in_specs, out_specs=out_specs, check_vma=False)
```

time: 1080 us -> 727 us (0.67)
  waiting for transfers between devices: 678 us -> 114 us
  Pallas kernels: 0 us -> 379 us
  matrix products: 95.7 us -> 8.28 us
  other arithmetic: 114 us -> 78.2 us
  starting transfers between devices: 97.5 us -> 63.6 us
    ppermute x44 -> x30, waiting for transfers between devices: 548 us -> 75.9 us  [the longest x17 75.9 us: send(): got = lax.ppermute(array, axis, pairs)]
    pallas_call x0 -> x10, Pallas kernels: none -> 379 us  [the longest x1 326 us: gather_and_sum(): pl.pallas_call(kernel, out_shape=[jax.ShapeDtypeStruct((counts[w], own_ro...]
    dot_general x33 -> x0, matrix products: 62.4 us -> none  [the longest x12 20.6 us: contract_first(): lax.dot_general(left, right, (((0,), (0,)), ((), ())), preferred_element_...]
    ppermute x9, waiting for transfers between devices: 46.8 us -> 0.02 us  [trade_blocks(): lax.ppermute(blocks[r], 'dp', xor_pairs(size, r))]
    concatenate x26 -> x17, other arithmetic: 62.7 us -> 22.8 us  [the longest x3 10 us: columns(): jnp.concatenate([stack[3 * n + which].astype(f32) for n in range(len(edge...]
    ppermute x8, waiting for transfers between devices: 40.4 us -> 8.42 us  [small_total(): vector = vector + lax.ppermute(vector, axis, xor_pairs(size, mask))]
    ppermute x44 -> x30, starting transfers between devices: 62 us -> 34.8 us  [the longest x17 29.5 us: send(): got = lax.ppermute(array, axis, pairs)]
    dot_general x17 -> x2, matrix products: 30 us -> 3.67 us  [contract_last(): lax.dot_general(left, right, (((1,), (1,)), ((), ())), preferred_element_...]
  transfers between devices with their start and end apart: 96 -> 58, of which waited for: 34 -> 22; matrix products, arithmetic and copies ran while one was open for 24% -> 19% of each run, Pallas kernels for 0% -> 53%
where the time goes in v2:
time: 727 us; the launch traced here: 720 us
  Pallas kernels  379 us (52%)
  waiting for transfers between devices  114 us (16%)
  other arithmetic  78.2 us (11%)
  local copies, waits for them, and re-layouts  73.6 us (10%)
  starting transfers between devices  63.6 us (9%)
  matrix products  8.28 us (1%)
    pallas_call x1, Pallas kernels, gather_and_sum(): pl.pallas_call(kernel, out_shape=[jax.ShapeDtypeStruct((counts[w], own_ro...  326 us
    ppermute x17, waiting for transfers between devices, send(): got = lax.ppermute(array, axis, pairs)  75.9 us
    pallas_call x7, Pallas kernels, feed_chunk(): pl.pallas_call(kernel, out_shape=(jax.ShapeDtypeStruct((rows, 3 * width),...  40.4 us
    unnamed x250, local copies, waits for them, and re-layouts  33 us
    ppermute x17, starting transfers between devices, send(): got = lax.ppermute(array, axis, pairs)  29.5 us
    ppermute x4, waiting for transfers between devices, tensor_sum(): other = lax.ppermute(sent, 'tensor', [(0, 1), (1, 0)])  26.3 us
  transfers between devices with their start and end apart: 58, of which 22 were waited for; matrix products, arithmetic and copies ran while one was open for 19% of the time, Pallas kernels for 53%

profile of v2, /device:TPU:0, one launch (start us, length us, event | category | flops | bytes accessed | tf_op | source)
XLA Modules:
  0.0 720.0 jit_solution(3854428493796362953)
XLA Ops:
  38.1 7.3 %collective-permute-done.7 = bf16[192,768]{1,0:T(8,128)(2,1)} collective-permute-done((bf16[192,768]{1,0:T(8,128)(2,1)S(1)}, bf16[192,768]{1,0:T(8,128)(2,1)}, u32[]{:S(2)}, u32[]{:S(2)}) %collective-permute-start.7) | collective-permute-done | bytes 294944 | tf_op jit(solution)/shard_map/ppermute | solution.py:29
  76.2 4.5 collective-permute-start.5
  91.2 4.2 collective-permute-start.21
  95.5 5.7 attend.1
  134.9 6.4 collective-permute-done.17
  153.1 4.9 collective-permute-done.18
  167.6 7.3 %collective-permute-done.19 = bf16[192,1920]{1,0:T(8,128)(2,1)S(1)} collective-permute-done((bf16[192,1920]{1,0:T(8,128)(2,1)}, bf16[192,1920]{1,0:T(8,128)(2,1)S(1)}, u32[]{:S(2)}, u32[]{:S(2)}) %collective-permute-start.19) | collective-permute-done | bytes 737312 | tf_op jit(solution)/shard_map/ppermute | solution.py:29
  188.3 6.1 collective-permute-done.26
  198.2 15.1 %collective-permute-done.27 = bf16[192,1920]{1,0:T(8,128)(2,1)S(1)} collective-permute-done((bf16[192,1920]{1,0:T(8,128)(2,1)S(1)}, bf16[192,1920]{1,0:T(8,128)(2,1)S(1)}, u32[]{:S(2)}, u32[]{:S(2)}) %collective-permute-start.27) | collective-permute-done | bytes 737312 | tf_op jit(solution)/shard_map/ppermute | solution.py:29
  214.8 5.6 feed_chunk.7
  221.4 5.6 feed_chunk.8
  228.6 5.7 feed_chunk.9
  236.7 5.7 feed_chunk.10
  242.6 6.0 feed_chunk.11
  249.5 5.7 feed_chunk.12
  255.3 6.1 feed_chunk.13
  274.8 11.7 %collective-permute-done.36 = bf16[256,1536]{0,1:T(8,128)(2,1)} collective-permute-done((bf16[256,1536]{0,1:T(8,128)(2,1)}, bf16[256,1536]{0,1:T(8,128)(2,1)}, u32[]{:S(2)}, u32[]{:S(2)}) %collective-permute-start.36) | collective-permute-done | bytes 786464 | tf_op jit(solution)/shard_map/ppermute | solution.py:89
  288.5 14.1 %collective-permute-done.35 = bf16[256,1536]{0,1:T(8,128)(2,1)S(1)} collective-permute-done((bf16[256,1536]{0,1:T(8,128)(2,1)S(1)}, bf16[256,1536]{0,1:T(8,128)(2,1)S(1)}, u32[]{:S(2)}, u32[]{:S(2)}) %collective-permute-start.35) | collective-permute-done | bytes 786464 | tf_op jit(solution)/shard_map/ppermute | solution.py:89
  302.6 6.4 fusion.53
  312.4 6.5 attend_back.1
  325.9 4.2 collective-permute-start.57
  333.4 4.6 collective-permute-done.57
  350.7 326.4 %gather_and_sum.1 = (bf16[21,384,640]{2,1,0:T(8,128)(2,1)}, bf16[2,384,896]{2,1,0:T(8,128)(2,1)}, bf16[3,8,256,1920]{3,2,1,0:T(8,128)(2,1)}) custom-call(bf16[256,1920]{1,0:T(8,128)(2,1)} %copy-done.11, bf16[256,1920]{1,0:T(8,128)(2,1)} %copy-done.12, bf16[256,1920]{1,0:T(8,128)(2,1)} %copy-done.13, bf16[256,1920]{1,0:T(8,128)(2,1)} %copy-done.14, ...), custom_call_target="tpu_custom_call" | custom-call | flops 11978932224 | bytes 101384192 | tf_op jit(solution)/shard_map/gather_and_sum/pallas_call | solution.py:616
  710.4 5.4 fusion.15
  (475 shorter events, 235.7 us)
Async XLA Ops:
  5.8 30.5 %collective-permute-start.1 = (bf16[384,1024]{1,0:T(8,128)(2,1)}, bf16[384,1024]{1,0:T(8,128)(2,1)}, u32[]{:S(2)}, u32[]{:S(2)}) collective-permute-start(bf16[384,1024]{1,0:T(8,128)(2,1)} %constant_dynamic-update-slice_fusion), channel_id=1, source_target_pairs={{0,16},{8,24},{16,0},{24,8},{1,17},{9,25},{17,1},{25,9},{2,18},{10... | collective-permute-start | bytes 2359304 | tf_op jit(solution)/shard_map/ppermute | solution.py:29
  8.7 53.8 %collective-permute-start = (bf16[384,1024]{1,0:T(8,128)(2,1)}, bf16[384,1024]{1,0:T(8,128)(2,1)}, u32[]{:S(2)}, u32[]{:S(2)}) collective-permute-start(bf16[384,1024]{1,0:T(8,128)(2,1)} %constant_dynamic-update-slice_fusion), channel_id=1, source_target_pairs={{0,8},{8,0},{16,24},{24,16},{1,9},{9,1},{17,25},{25,17},{2,10},{10... | collective-permute-start | bytes 2359304 | tf_op jit(solution)/shard_map/ppermute | solution.py:75
  8.7 46.7 %collective-permute-start.6 = (bf16[384,768]{1,0:T(8,128)(2,1)}, bf16[384,768]{1,0:T(8,128)(2,1)}, u32[]{:S(2)}, u32[]{:S(2)}) collective-permute-start(bf16[384,768]{1,0:T(8,128)(2,1)} %param.24), channel_id=1, source_target_pairs={{0,8},{8,0},{16,24},{24,16},{1,9},{9,1},{17,25},{25,17},{2,10},{10... | collective-permute-start | bytes 1769480 | tf_op jit(solution)/shard_map/ppermute | solution.py:75
  57.3 32.3 %collective-permute-start.14 = (bf16[192,1920]{1,0:T(8,128)(2,1)}, bf16[192,1920]{1,0:T(8,128)(2,1)}, u32[]{:S(2)}, u32[]{:S(2)}) collective-permute-start(bf16[192,1920]{1,0:T(8,128)(2,1)} %fusion.31), channel_id=1, source_target_pairs={{0,16},{8,24},{16,0},{24,8},{1,17},{9,25},{17,1},{25,9},{2,18},{10... | collective-permute-start | bytes 2211848 | tf_op jit(solution)/shard_map/ppermute | solution.py:29
  62.3 38.9 %collective-permute-start.9 = (bf16[384,768]{1,0:T(8,128)(2,1)}, bf16[384,768]{1,0:T(8,128)(2,1)}, u32[]{:S(2)}, u32[]{:S(2)}) collective-permute-start(bf16[384,768]{1,0:T(8,128)(2,1)} %pad_maximum_fusion.15), channel_id=1, source_target_pairs={{0,8},{8,0},{16,24},{24,16},{1,9},{9,1},{17,25},{25,17},{2,10},{10... | collective-permute-start | bytes 1769480 | tf_op jit(solution)/shard_map/ppermute | solution.py:75
  86.0 108.4 %collective-permute-start.11 = (bf16[384,4480]{1,0:T(8,128)(2,1)S(1)}, bf16[384,4480]{1,0:T(8,128)(2,1)}, u32[]{:S(2)}, u32[]{:S(2)}) collective-permute-start(bf16[384,4480]{1,0:T(8,128)(2,1)S(1)} %copy-done), channel_id=1, source_target_pairs={{0,8},{8,0},{16,24},{24,16},{1,9},{9,1},{17,25},{25,17},{2,10},{10... | collective-permute-start | bytes 10321928 | tf_op jit(solution)/shard_map/ppermute | solution.py:708
  87.4 110.0 %collective-permute-start.12 = (bf16[384,4480]{1,0:T(8,128)(2,1)}, bf16[384,4480]{1,0:T(8,128)(2,1)}, u32[]{:S(2)}, u32[]{:S(2)}) collective-permute-start(bf16[384,4480]{1,0:T(8,128)(2,1)} %refs_3_.13), channel_id=1, source_target_pairs={{0,8},{8,0},{16,24},{24,16},{1,9},{9,1},{17,25},{25,17},{2,10},{10... | collective-permute-start | bytes 10321928 | tf_op jit(solution)/shard_map/ppermute | solution.py:708
  91.2 20.9 %collective-permute-start.21 = (bf16[192,1920]{1,0:T(8,128)(2,1)}, bf16[192,1920]{1,0:T(8,128)(2,1)S(1)}, u32[]{:S(2)}, u32[]{:S(2)}) collective-permute-start(bf16[192,1920]{1,0:T(8,128)(2,1)} %collective-permute-done.14), channel_id=1, source_target_pairs={{0,2},{2,0},{4,6},{6,4},{1,3},{3,1},{5,7},{7,5},{8,10},{10,8},{12,... | collective-permute-start | bytes 2211848 | tf_op jit(solution)/shard_map/ppermute | solution.py:29
  133.3 64.5 %collective-permute-start.13 = (bf16[384,4480]{1,0:T(8,128)(2,1)}, bf16[384,4480]{1,0:T(8,128)(2,1)}, u32[]{:S(2)}, u32[]{:S(2)}) collective-permute-start(bf16[384,4480]{1,0:T(8,128)(2,1)} %refs_4_.13), channel_id=1, source_target_pairs={{0,8},{8,0},{16,24},{24,16},{1,9},{9,1},{17,25},{25,17},{2,10},{10... | collective-permute-start | bytes 10321928 | tf_op jit(solution)/shard_map/ppermute | solution.py:708
  188.3 25.2 %collective-permute-start.33 = (bf16[384,1920]{1,0:T(8,128)(2,1)S(1)}, bf16[384,1920]{1,0:T(8,128)(2,1)S(1)}, u32[]{:S(2)}, u32[]{:S(2)}) collective-permute-start(bf16[384,1920]{1,0:T(8,128)(2,1)S(1)} %pad_maximum_fusion.6.refs_8_), channel_id=1, source_target_pairs={{0,8},{8,0},{16,24},{24,16},{1,9},{9,1},{17,25},{25,17},{2,10},{10... | collective-permute-start | bytes 4423688 | tf_op jit(solution)/shard_map/ppermute | solution.py:720
  197.5 30.5 %collective-permute-start.32 = (bf16[384,1920]{1,0:T(8,128)(2,1)S(1)}, bf16[384,1920]{1,0:T(8,128)(2,1)}, u32[]{:S(2)}, u32[]{:S(2)}) collective-permute-start(bf16[384,1920]{1,0:T(8,128)(2,1)S(1)} %pad_maximum_fusion.5.refs_8_), channel_id=1, source_target_pairs={{0,8},{8,0},{16,24},{24,16},{1,9},{9,1},{17,25},{25,17},{2,10},{10... | collective-permute-start | bytes 4423688 | tf_op jit(solution)/shard_map/ppermute | solution.py:720
  197.9 37.4 %collective-permute-start.31 = (bf16[384,1920]{1,0:T(8,128)(2,1)S(1)}, bf16[384,1920]{1,0:T(8,128)(2,1)}, u32[]{:S(2)}, u32[]{:S(2)}) collective-permute-start(bf16[384,1920]{1,0:T(8,128)(2,1)S(1)} %pad_maximum_fusion.4.refs_8_), channel_id=1, source_target_pairs={{0,8},{8,0},{16,24},{24,16},{1,9},{9,1},{17,25},{25,17},{2,10},{10... | collective-permute-start | bytes 4423688 | tf_op jit(solution)/shard_map/ppermute | solution.py:720
  213.3 29.2 %collective-permute-start.30 = (bf16[384,1920]{1,0:T(8,128)(2,1)S(1)}, bf16[384,1920]{1,0:T(8,128)(2,1)}, u32[]{:S(2)}, u32[]{:S(2)}) collective-permute-start(bf16[384,1920]{1,0:T(8,128)(2,1)S(1)} %pad_maximum_fusion.3.refs_8_), channel_id=1, source_target_pairs={{0,8},{8,0},{16,24},{24,16},{1,9},{9,1},{17,25},{25,17},{2,10},{10... | collective-permute-start | bytes 4423688 | tf_op jit(solution)/shard_map/ppermute | solution.py:720
  213.5 36.0 %collective-permute-start.29 = (bf16[384,1920]{1,0:T(8,128)(2,1)S(1)}, bf16[384,1920]{1,0:T(8,128)(2,1)}, u32[]{:S(2)}, u32[]{:S(2)}) collective-permute-start(bf16[384,1920]{1,0:T(8,128)(2,1)S(1)} %pad_maximum_fusion.2.refs_8_), channel_id=1, source_target_pairs={{0,8},{8,0},{16,24},{24,16},{1,9},{9,1},{17,25},{25,17},{2,10},{10... | collective-permute-start | bytes 4423688 | tf_op jit(solution)/shard_map/ppermute | solution.py:720
  214.2 41.1 %collective-permute-start.28 = (bf16[384,1920]{1,0:T(8,128)(2,1)S(1)}, bf16[384,1920]{1,0:T(8,128)(2,1)}, u32[]{:S(2)}, u32[]{:S(2)}) collective-permute-start(bf16[384,1920]{1,0:T(8,128)(2,1)S(1)} %pad_maximum_fusion.1.refs_8_), channel_id=1, source_target_pairs={{0,8},{8,0},{16,24},{24,16},{1,9},{9,1},{17,25},{25,17},{2,10},{10... | collective-permute-start | bytes 4423688 | tf_op jit(solution)/shard_map/ppermute | solution.py:720
  227.9 39.4 %collective-permute-start.50 = (bf16[256,768]{0,1:T(8,128)(2,1)}, bf16[256,768]{0,1:T(8,128)(2,1)}, u32[]{:S(2)}, u32[]{:S(2)}) collective-permute-start(bf16[256,768]{0,1:T(8,128)(2,1)} %pad_maximum_fusion.22), channel_id=1, source_target_pairs={{0,24},{8,16},{16,8},{24,0},{1,25},{9,17},{17,9},{25,1},{2,26},{10... | collective-permute-start | bytes 1179656 | tf_op jit(solution)/shard_map/ppermute | solution.py:81
  235.3 32.1 %collective-permute-start.49 = (bf16[256,768]{0,1:T(8,128)(2,1)}, bf16[256,768]{0,1:T(8,128)(2,1)}, u32[]{:S(2)}, u32[]{:S(2)}) collective-permute-start(bf16[256,768]{0,1:T(8,128)(2,1)} %pad_maximum_fusion.21), channel_id=1, source_target_pairs={{0,16},{8,24},{16,0},{24,8},{1,17},{9,25},{17,1},{25,9},{2,18},{10... | collective-permute-start | bytes 1179656 | tf_op jit(solution)/shard_map/ppermute | solution.py:81
  242.5 24.8 %collective-permute-start.48 = (bf16[256,768]{0,1:T(8,128)(2,1)}, bf16[256,768]{0,1:T(8,128)(2,1)}, u32[]{:S(2)}, u32[]{:S(2)}) collective-permute-start(bf16[256,768]{0,1:T(8,128)(2,1)} %pad_maximum_fusion.20), channel_id=1, source_target_pairs={{0,8},{8,0},{16,24},{24,16},{1,9},{9,1},{17,25},{25,17},{2,10},{10... | collective-permute-start | bytes 1179656 | tf_op jit(solution)/shard_map/ppermute | solution.py:81
  270.4 32.1 %collective-permute-start.35 = (bf16[256,1536]{0,1:T(8,128)(2,1)S(1)}, bf16[256,1536]{0,1:T(8,128)(2,1)S(1)}, u32[]{:S(2)}, u32[]{:S(2)}) collective-permute-start(bf16[256,1536]{0,1:T(8,128)(2,1)S(1)} %pad_maximum_fusion.12), channel_id=1, source_target_pairs={{0,1},{1,0},{2,3},{3,2},{4,5},{5,4},{6,7},{7,6},{8,9},{9,8},{10,11... | collective-permute-start | bytes 2359304 | tf_op jit(solution)/shard_map/ppermute | solution.py:89
  272.9 51.7 %collective-permute-start.45 = (bf16[256,384]{0,1:T(8,128)(2,1)S(1)}, bf16[256,384]{0,1:T(8,128)(2,1)S(1)}, u32[]{:S(2)}, u32[]{:S(2)}) collective-permute-start(bf16[256,384]{0,1:T(8,128)(2,1)S(1)} %copy-done.83), channel_id=1, source_target_pairs={{0,8},{8,0},{16,24},{24,16},{1,9},{9,1},{17,25},{25,17},{2,10},{10... | collective-permute-start | bytes 589832 | tf_op jit(solution)/shard_map/ppermute | solution.py:81
  272.9 52.9 %collective-permute-start.46 = (bf16[256,384]{0,1:T(8,128)(2,1)S(1)}, bf16[256,384]{0,1:T(8,128)(2,1)S(1)}, u32[]{:S(2)}, u32[]{:S(2)}) collective-permute-start(bf16[256,384]{0,1:T(8,128)(2,1)S(1)} %copy-done.81), channel_id=1, source_target_pairs={{0,16},{8,24},{16,0},{24,8},{1,17},{9,25},{17,1},{25,9},{2,18},{10... | collective-permute-start | bytes 589832 | tf_op jit(solution)/shard_map/ppermute | solution.py:81
  273.5 56.5 %collective-permute-start.47 = (bf16[256,384]{0,1:T(8,128)(2,1)S(1)}, bf16[256,384]{0,1:T(8,128)(2,1)S(1)}, u32[]{:S(2)}, u32[]{:S(2)}) collective-permute-start(bf16[256,384]{0,1:T(8,128)(2,1)S(1)} %copy-done.79), channel_id=1, source_target_pairs={{0,24},{8,16},{16,8},{24,0},{1,25},{9,17},{17,9},{25,1},{2,26},{10... | collective-permute-start | bytes 589832 | tf_op jit(solution)/shard_map/ppermute | solution.py:81
  288.4 23.4 %collective-permute-start.54 = (f32[1536]{0:T(1024)S(1)}, f32[1536]{0:T(1024)S(1)}, u32[]{:S(2)}, u32[]{:S(2)}) collective-permute-start(f32[1536]{0:T(1024)S(1)} %get-tuple-element.128), channel_id=1, source_target_pairs={{0,8},{8,0},{16,24},{24,16},{1,9},{9,1},{17,25},{25,17},{2,10},{10... | collective-permute-start | bytes 18440 | tf_op jit(solution)/shard_map/ppermute | solution.py:111
  346.3 342.3 %collective-permute-start.40 = (bf16[256,1536]{0,1:T(8,128)(2,1)}, bf16[256,1536]{0,1:T(8,128)(2,1)}, u32[]{:S(2)}, u32[]{:S(2)}) collective-permute-start(bf16[256,1536]{0,1:T(8,128)(2,1)} %pad_maximum_fusion.14), channel_id=1, source_target_pairs={{0,1},{1,0},{2,3},{3,2},{4,5},{5,4},{6,7},{7,6},{8,9},{9,8},{10,11... | collective-permute-start | bytes 2359304 | tf_op jit(solution)/shard_map/ppermute | solution.py:89
  (152 other events, 1850.2 us)

commit v3 on v2

--- a/solution.py
+++ b/solution.py
@@ -644,6 +644,617 @@
     return [(results[kind], index) for _, _, kind, index in where]
 
 
+def layer_back(
+    length, hidden, tokens, grad_out, gains, feed_own, feed_near, feed_far, out_pieces, pair_pieces,
+    query, pair, lse, mixed, cosine, sine,
+):
+    bf16, f32 = jnp.bfloat16, jnp.float32
+    rows, features = hidden.shape
+    own_rows = feed_own[0].shape[0]
+    chunks = len(feed_far)
+    width = feed_far[0][0].shape[1] // 3
+    heads_width = query.shape[1]
+    heads = heads_width // HEAD_DIM
+    keys = pair.shape[0]
+    pair_width = pair.shape[1]
+    projected = heads_width + pair_width
+    last_width = projected + heads_width
+    halfway = last_width // 2
+    size = features // own_rows
+    units = chunks + 1
+    tokens_all = size * rows
+    small_width = 2 * features + projected
+    scale = 1.0 / math.sqrt(HEAD_DIM)
+    part = 64
+    where = []
+    for k in range(chunks):
+        where.append((k, [(0, 0, width)], 0, 3 * k))
+        where.append((k, [(0, width, width)], 0, 3 * k + 1))
+        where.append((k, [(1, 2 * width, width)], 0, 3 * k + 2))
+    where.append((chunks, [(2, 0, halfway)], 1, 0))
+    where.append(
+        (chunks, [(2, halfway, projected - halfway), (3, projected, heads_width)], 1, 1)
+    )
+    count = len(where)
+    widths = (width, halfway)
+    far_flat = [a for pieces in feed_far for a in pieces]
+
+    def kernel(*refs):
+        refs = list(refs)
+
+        def take(n):
+            taken = refs[:n]
+            del refs[:n]
+            return taken
+
+        (length_ref, gains_ref, lse_ref, cos_ref, sin_ref) = take(5)
+        (hidden_hbm, tokens_hbm, grad_hbm, query_hbm, pair_hbm, mixed_hbm) = take(6)
+        own_hbm, near_hbm, far_hbm = take(3), take(3), take(2 * chunks)
+        out_hbm, pairw_hbm = take(size), take(size)
+        output_hbm, grad_tokens_hbm, small_ref, sum_wide, sum_last, land, acts_hbm, across_wide, across_last = take(9)
+        (mine_wide, mine_last, stage_in, stage_across, table, weights, feature_t, feature_land) = take(8)
+        (row_two, row_fall, row_normed, row_branch, hidden_rel, tokens_rel, d_sum, out_sum) = take(8)
+        (y_send, y_land, acts_stage, query_v, pair_v, last_v, bias, key_t, d_key, d_value) = take(10)
+        (d_mixed, d_rest, d_land, vec, vec_land, total_land) = take(6)
+        (s_in, s_weights, s_acts, s_rest, send_g, recv_g, send_a, recv_a, send_b, recv_b) = take(10)
+        (s_stage, s_keep, s_table, send_t, recv_t, send_y, recv_y, send_k, recv_k) = take(9)
+        (send_v, recv_v, send_w, recv_w, s_store) = take(5)
+        sums, mines, acrosses = (sum_wide, sum_last), (mine_wide, mine_last), (across_wide, across_last)
+        rows_of = (row_two, row_fall, row_normed, row_branch)
+
+        me = lax.axis_index("dp")
+        place = lax.axis_index("context")
+        side = lax.axis_index("tensor")
+        middle = place * (3 - place) == 2
+        inner = 1 + place // 2
+        across = 3 - place
+        outer = 3 * (place - 1)
+        one = flipped(me, 1)
+        partner = (me, one, flipped(me, 2), flipped(one, 2))
+
+        barrier = pltpu.get_barrier_semaphore()
+        for r in range(1, size):
+            pl.semaphore_signal(barrier, 1, device_id={"dp": partner[r]}, device_id_type=MESH)
+        for s in range(1, 4):
+            pl.semaphore_signal(barrier, 1, device_id={"context": lax.rem(place + s, 4)}, device_id_type=MESH)
+        pl.semaphore_signal(barrier, 1, device_id={"tensor": 1 - side}, device_id_type=MESH)
+
+        def block_of(r):
+            return pl.ds(pl.multiple_of(partner[r] * own_rows, 128), own_rows)
+
+        def local(source, target, sem):
+            return pltpu.make_async_copy(source, target, sem)
+
+        def remote(source, target, send, recv, axis, index):
+            return pltpu.make_async_remote_copy(
+                src_ref=source, dst_ref=target, send_sem=send, recv_sem=recv,
+                device_id={axis: index}, device_id_type=MESH,
+            )
+
+        def cols(r):
+            return pl.ds(r * own_rows, own_rows)
+
+        ins = []
+        for n, (source, target) in enumerate(
+            ((hidden_hbm, hidden_rel), (grad_hbm, row_fall), (tokens_hbm, tokens_rel))
+        ):
+            ins.append(
+                [local(source.at[:, block_of(r)], target.at[:, cols(r)], s_in.at[n, r]) for r in range(size)]
+            )
+        rest = [
+            local(query_hbm, query_v, s_rest.at[0]),
+            local(pair_hbm, pair_v, s_rest.at[1]),
+            local(mixed_hbm, last_v.at[:, pl.ds(projected, heads_width)], s_rest.at[2]),
+        ]
+
+        def weight_copies(k, which):
+            view = pl.ds(which * width, width)
+            sources = [
+                own_hbm[which].at[:, pl.ds(k * width, width)],
+                near_hbm[which].at[:, pl.ds(k * width, width)],
+                far_hbm[2 * k].at[:, view],
+                far_hbm[2 * k + 1].at[:, view],
+            ]
+            return [
+                local(source, weights.at[pl.ds(r * own_rows, own_rows), view], s_weights.at[which, r])
+                for r, source in enumerate(sources)
+            ]
+
+        def side_copies():
+            return [
+                local(out_hbm[r], weights.at[pl.ds(r * own_rows, own_rows), pl.ds(0, heads_width)], s_weights.at[0, r])
+                for r in range(size)
+            ] + [
+                local(pairw_hbm[r], weights.at[pl.ds(r * own_rows, own_rows), pl.ds(heads_width, projected)], s_weights.at[1, r])
+                for r in range(size)
+            ]
+
+        def start(copies):
+            for copy in copies:
+                copy.start()
+
+        def wait(copies):
+            for copy in copies:
+                copy.wait()
+
+        for copies in ins:
+            start(copies)
+        for which in range(3):
+            start(weight_copies(0, which))
+        start(rest)
+
+        def trade(w, r):
+            return remote(
+                rows_of[w].at[:, cols(r)], feature_land.at[w, r - 1], send_t.at[w, r - 1], recv_t.at[w, r - 1],
+                "dp", partner[r],
+            )
+
+        def turn_features(w):
+            feature_t[w, :, 0:rows] = rows_of[w][:, 0:own_rows].T
+            for r in range(1, size):
+                trade(w, r).wait_recv()
+                feature_t[w, :, r * rows : (r + 1) * rows] = feature_land[w, r - 1].T
+
+        steps = ((0, 2), (0, 1), (2, 1))
+
+        def unit_width(u):
+            return 3 * width if u < chunks else last_width
+
+        def piece(u, r):
+            view = pl.ds(0, unit_width(u))
+            return acts_hbm.at[u, :, view] if r == 0 else land.at[r - 1, u, :, view]
+
+        def transfer(u, n):
+            r, mask = steps[n]
+            return remote(
+                piece(u, r), land.at[(r ^ mask) - 1, u, :, pl.ds(0, unit_width(u))],
+                send_g.at[n, u], recv_g.at[n, u], "dp", partner[mask],
+            )
+
+        def own_copy(u):
+            if u < chunks:
+                return local(acts_stage.at[u % 2], piece(u, 0), s_acts.at[u])
+            return local(last_v, piece(u, 0), s_acts.at[u])
+
+        def begin(u):
+            own_copy(u).wait()
+            transfer(u, 0).start()
+            transfer(u, 1).start()
+
+        def table_copies(u):
+            return [
+                local(
+                    piece(u, r), table.at[pl.ds(r * rows, rows), pl.ds(0, unit_width(u))], s_table.at[r]
+                )
+                for r in range(size)
+            ]
+
+        def hop(j, source, target, to, send, recv):
+            _, _, kind, index = where[j]
+            return remote(
+                source[kind].at[index], target[kind].at[index], send.at[j], recv.at[j], "context", to
+            )
+
+        def hop_in(j):
+            return hop(j, mines, sums, inner, send_a, recv_a)
+
+        def hop_across(j):
+            return hop(j, mines, acrosses, across, send_b, recv_b)
+
+        def hop_out(j):
+            return hop(j, mines, sums, outer, send_a, recv_a)
+
+        def staged(j, source, stage, n):
+            _, _, kind, index = where[j]
+            return local(
+                source[kind].at[index], stage.at[j % 2, :, pl.ds(0, widths[kind])], s_stage.at[n, j % 2]
+            )
+
+        def keep(j):
+            _, _, kind, index = where[j]
+            return local(mines[kind].at[index], sums[kind].at[index], s_keep.at[j])
+
+        def add_stage(j, stage):
+            _, _, kind, index = where[j]
+            mines[kind][index] = (
+                mines[kind][index].astype(f32) + stage[j % 2, :, 0 : widths[kind]].astype(f32)
+            ).astype(bf16)
+
+        def line_step(j):
+            if j < count:
+                hop_in(j).wait_recv()
+                staged(j, sums, stage_in, 0).start()
+            if j >= 1:
+                hop_across(j - 1).wait_recv()
+                staged(j - 1, acrosses, stage_across, 1).start()
+            if j < count:
+                staged(j, sums, stage_in, 0).wait()
+                add_stage(j, stage_in)
+                hop_across(j).start()
+            if j >= 1:
+                staged(j - 1, acrosses, stage_across, 1).wait()
+                hop_across(j - 1).wait_send()
+                add_stage(j - 1, stage_across)
+                hop_out(j - 1).start()
+                keep(j - 1).start()
+
+        of_unit = [[j for j in range(count) if where[j][0] == u] for u in range(units)]
+
+        def gradients(u):
+            transfer(u, 0).wait_recv()
+            transfer(u, 2).start()
+            transfer(u, 1).wait_recv()
+            transfer(u, 2).wait_recv()
+            start(table_copies(u))
+            wait(table_copies(u))
+            for j in of_unit[u]:
+                _, spans, kind, index = where[j]
+                filled = 0
+                for which, at, w in spans:
+                    mines[kind][index, :, filled : filled + w] = dot_nn(
+                        feature_t[which], table[:, at : at + w]
+                    ).astype(bf16)
+                    filled += w
+
+                @pl.when(jnp.logical_not(middle))
+                def _(j=j):
+                    if j >= 3:
+                        hop_in(j - 3).wait_send()
+                    hop_in(j).start()
+
+        def line(u):
+            @pl.when(middle)
+            def _():
+                for j in of_unit[u]:
+                    line_step(j)
+
+        def feed(k):
+            if k >= 2:
+                own_copy(k - 2).wait() if k - 2 >= begun[0] else None
+            wait(weight_copies(k, 0))
+            gate_w, up_w, down_w = (weights.at[:, pl.ds(n * width, width)] for n in range(3))
+            gate = dot_nn(row_two[...], gate_w[...])
+            wait(weight_copies(k, 1))
+            up = dot_nn(row_two[...], up_w[...])
+            wait(weight_copies(k, 2))
+            d_active = dot_nn(row_fall[...], down_w[...])
+            sigmoid = jax.nn.sigmoid(gate)
+            swish = gate * sigmoid
+            stage = acts_stage.at[k % 2]
+            stage[:, 2 * width :] = (swish * up).astype(bf16)
+            stage[:, :width] = (d_active * up * sigmoid * (1.0 + gate * (1.0 - sigmoid))).astype(bf16)
+            stage[:, width : 2 * width] = (d_active * swish).astype(bf16)
+            own_copy(k).start()
+            d_part = contract_last(stage[:, :width], gate_w[...]) + contract_last(
+                stage[:, width : 2 * width], up_w[...]
+            )
+            out_part = contract_last(stage[:, 2 * width :], down_w[...])
+            if k == 0:
+                d_sum[...] = d_part
+                out_sum[...] = out_part
+            else:
+                d_sum[...] += d_part
+                out_sum[...] += out_part
+            if k + 1 < chunks:
+                for which in range(3):
+                    start(weight_copies(k + 1, which))
+            else:
+                start(side_copies())
+
+        def swap(n):
+            return remote(y_send.at[n], y_land.at[n], send_y.at[n], recv_y.at[n], "tensor", 1 - side)
+
+        gain_one, gain_two = gains_ref[0:1, :], gains_ref[1:2, :]
+
+        def mean_scale(field):
+            return lax.rsqrt(jnp.mean(field * field, -1, keepdims=True) + EPSILON)
+
+        spans_of_rows = [slice(n, n + part) for n in range(0, rows, part)]
+
+        def row_valid(span):
+            at = lax.broadcasted_iota(jnp.int32, (part, 1), 0) + (place * rows + span.start)
+            return (at < length_ref[0]).astype(f32)
+
+        def keep_gain(which, value):
+            for r in range(size):
+                at = pl.multiple_of(partner[r] * own_rows + which * features, 128)
+                vec[:, pl.ds(at, own_rows)] = value[:, r * own_rows : (r + 1) * own_rows]
+
+        wait(ins[0])
+        for span in spans_of_rows:
+            field = hidden_rel[span, :]
+            row_two[span, :] = (field * mean_scale(field) * gain_two).astype(bf16)
+        wait(ins[1])
+        for span in spans_of_rows:
+            row_fall[span, :] = (row_fall[span, :].astype(f32) * row_valid(span)).astype(bf16)
+        pl.semaphore_wait(barrier, size - 1 + 3 + 1)
+        for r in (2, 3, 1):
+            for w in (0, 1):
+                trade(w, r).start()
+        begun = [0]
+
+        feed(0)
+        begin(0)
+        begun[0] = 1
+        feed(1)
+        begin(1)
+        begun[0] = 2
+        wait(ins[2])
+        for span in spans_of_rows:
+            field = tokens_rel[span, :].astype(f32)
+            row_normed[span, :] = (field * mean_scale(field) * gain_one).astype(bf16)
+        turn_features(0)
+        turn_features(1)
+        feed(2)
+        feed(3)
+        gradients(0)
+        begin(2)
+        begin(3)
+        begun[0] = 4
+        feed(4)
+        feed(5)
+        line(0)
+        gradients(1)
+        begin(4)
+        begun[0] = 5
+        feed(6)
+        y_send[0] = d_sum[...].astype(bf16)
+        swap(0).start()
+        y_send[1] = out_sum[...].astype(bf16)
+        line(1)
+        swap(1).start()
+        for r in (2, 3, 1):
+            trade(2, r).start()
+        gradients(2)
+        begin(5)
+        swap(0).wait_recv()
+        gain_sum = jnp.zeros((1, features), f32)
+        for span in spans_of_rows:
+            d_normed = y_send[0, span, :].astype(f32) + y_land[0, span, :].astype(f32)
+            field = hidden_rel[span, :]
+            r2 = mean_scale(field)
+            gain_sum = gain_sum + jnp.sum(d_normed * field * r2, 0, keepdims=True)
+            weighted = d_normed * gain_two
+            d_hidden = (
+                row_fall[span, :].astype(f32)
+                + r2 * weighted
+                - field * (r2 * r2 * r2) * jnp.mean(field * weighted, -1, keepdims=True)
+            )
+            d_sum[span, :] = d_hidden
+            row_branch[span, :] = d_hidden.astype(bf16)
+        keep_gain(1, gain_sum)
+        for r in (2, 3, 1):
+            trade(3, r).start()
+        wait(side_copies())
+        d_mixed[...] = dot_nn(row_branch[...], weights[:, 0:heads_width]).astype(bf16)
+        line(2)
+        gradients(3)
+        begin(6)
+        wait(rest)
+        bias[...] = key_bias_table(place, length_ref[0], keys, rows)
+        key_t[...] = pair_v[:, :HEAD_DIM].T
+        for head in range(heads):
+            at = slice(head * HEAD_DIM, (head + 1) * HEAD_DIM)
+            scores = contract_last(pair_v[:, :HEAD_DIM], query_v[:, at]) * scale + bias[...]
+            probs = jnp.exp(scores - lse_ref[head : head + 1, :])
+            d_probs = contract_last(pair_v[:, HEAD_DIM:], d_mixed[:, at])
+            inside = jnp.sum(d_probs * probs, 0, keepdims=True)
+            d_scores = (probs * (d_probs - inside)).astype(bf16)
+            d_query = (dot_nn(key_t[...], d_scores) * scale).T
+            last_v[:, at] = turn(d_query, cos_ref[...], -sin_ref[...]).astype(bf16)
+            more_key = dot_nn(d_scores, query_v[:, at])
+            more_value = dot_nn(probs.astype(bf16), d_mixed[:, at])
+            if head == 0:
+                d_key[...] = more_key
+                d_value[...] = more_value
+            else:
+                d_key[...] += more_key
+                d_value[...] += more_value
+        d_rest[:, :HEAD_DIM] = (d_key[rows:, :] * scale).astype(bf16)
+        d_rest[:, HEAD_DIM:] = d_value[rows:, :].astype(bf16)
+
+        def give(s):
+            return remote(
+                d_rest.at[pl.ds((s - 1) * rows, rows), :], d_land.at[s - 1], send_k.at[s - 1], recv_k.at[s - 1],
+                "context", place - s,
+            )
+
+        for s in range(1, 4):
+            pl.when(place >= s)(give(s).start)
+        line(3)
+        gradients(4)
+        d_key[0:rows, :] = d_key[0:rows, :] * scale
+        for s in range(1, 4):
+
+            @pl.when(place + s <= 3)
+            def _(s=s):
+                give(s).wait_recv()
+                d_key[0:rows, :] += d_land[s - 1, :, :HEAD_DIM].astype(f32)
+                d_value[0:rows, :] += d_land[s - 1, :, HEAD_DIM:].astype(f32)
+
+        last_v[:, heads_width : heads_width + HEAD_DIM] = turn(
+            d_key[0:rows, :], cos_ref[...], -sin_ref[...]
+        ).astype(bf16)
+        last_v[:, heads_width + HEAD_DIM : projected] = d_value[0:rows, :].astype(bf16)
+        own_copy(chunks).start()
+        y_send[2] = contract_last(
+            last_v[:, 0:projected], weights[:, heads_width : heads_width + projected]
+        ).astype(bf16)
+        swap(2).start()
+        vec[:, 2 * features :] = jnp.sum(last_v[:, 0:projected].astype(f32), 0, keepdims=True)
+        begin(chunks)
+        turn_features(2)
+        turn_features(3)
+        swap(1).wait_recv()
+        swap(1).wait_send()
+        for span in spans_of_rows:
+            whole = y_send[1, span, :].astype(f32) + y_land[1, span, :].astype(f32)
+            y_land[1, span, :] = (row_valid(span) * (hidden_rel[span, :] + whole)).astype(bf16)
+
+        def stored(n, target):
+            return [
+                local(y_land.at[n, :, cols(r)], target.at[:, block_of(r)], s_store.at[n, r]) for r in range(size)
+            ]
+
+        start(stored(1, output_hbm))
+        line(4)
+        gradients(5)
+        swap(2).wait_recv()
+        swap(2).wait_send()
+        gain_sum = jnp.zeros((1, features), f32)
+        for span in spans_of_rows:
+            d_normed = y_send[2, span, :].astype(f32) + y_land[2, span, :].astype(f32)
+            field = tokens_rel[span, :].astype(f32)
+            r1 = mean_scale(field)
+            gain_sum = gain_sum + jnp.sum(d_normed * field * r1, 0, keepdims=True)
+            weighted = d_normed * gain_one
+            y_land[2, span, :] = (
+                d_sum[span, :]
+                + r1 * weighted
+                - field * (r1 * r1 * r1) * jnp.mean(field * weighted, -1, keepdims=True)
+            ).astype(bf16)
+        start(stored(2, grad_tokens_hbm))
+        keep_gain(0, gain_sum)
+
+        def share(r):
+            return remote(vec, vec_land.at[me], send_v.at[r - 1], recv_v.at[r - 1], "dp", partner[r])
+
+        def spread(s):
+            return remote(
+                vec, total_land.at[place], send_w.at[s - 1], recv_w.at[s - 1], "context", lax.rem(place + s, 4)
+            )
+
+        for r in range(1, size):
+            share(r).start()
+        vec_land[me] = vec[...]
+        line(5)
+        gradients(6)
+        for r in range(1, size):
+            share(r).wait()
+        vec[...] = vec_land[0] + vec_land[1] + vec_land[2] + vec_land[3]
+        for s in range(1, 4):
+            spread(s).start()
+        total_land[place] = vec[...]
+        line(6)
+        gradients(7)
+        for s in range(1, 4):
+            spread(s).wait()
+        small_ref[...] = total_land[0] + total_land[1] + total_land[2] + total_land[3]
+        line(7)
+
+        @pl.when(middle)
+        def _():
+            line_step(count)
+            for j in range(count):
+                hop_out(j).wait_send()
+                keep(j).wait()
+
+        @pl.when(jnp.logical_not(middle))
+        def _():
+            for j in range(count - 3, count):
+                hop_in(j).wait_send()
+            for j in range(count):
+                hop_out(j).wait_recv()
+
+        wait(stored(1, output_hbm))
+        wait(stored(2, grad_tokens_hbm))
+        swap(0).wait_send()
+        for s in range(1, 4):
+            pl.when(place >= s)(give(s).wait_send)
+        for w in range(4):
+            for r in range(1, size):
+                trade(w, r).wait_send()
+        for u in range(units):
+            for n in range(3):
+                transfer(u, n).wait_send()
+
+    dma = pltpu.SemaphoreType.DMA
+    shape = jax.ShapeDtypeStruct
+    wide, last = (3 * chunks, own_rows, width), (2, own_rows, halfway)
+    results = pl.pallas_call(
+        kernel,
+        out_shape=(
+            shape((rows, features), bf16),
+            shape((rows, features), bf16),
+            shape((1, small_width), f32),
+            shape(wide, bf16),
+            shape(last, bf16),
+            shape((size - 1, units, rows, 3 * width), bf16),
+            shape((units, rows, 3 * width), bf16),
+            shape(wide, bf16),
+            shape(last, bf16),
+        ),
+        in_specs=[SMEM, VMEM, VMEM, VMEM, VMEM] + [ANY] * (6 + 6 + 2 * chunks + 2 * size),
+        out_specs=(ANY, ANY, VMEM) + (ANY,) * 6,
+        scratch_shapes=[
+            pltpu.VMEM(wide, bf16),
+            pltpu.VMEM(last, bf16),
+            pltpu.VMEM((2, own_rows, max(widths)), bf16),
+            pltpu.VMEM((2, own_rows, max(widths)), bf16),
+            pltpu.VMEM((tokens_all, 3 * width), bf16),
+            pltpu.VMEM((features, 3 * width), bf16),
+            pltpu.VMEM((4, own_rows, tokens_all), bf16),
+            pltpu.VMEM((4, size - 1, rows, own_rows), bf16),
+            pltpu.VMEM((rows, features), bf16),
+            pltpu.VMEM((rows, features), bf16),
+            pltpu.VMEM((rows, features), bf16),
+            pltpu.VMEM((rows, features), bf16),
+            pltpu.VMEM((rows, features), f32),
+            pltpu.VMEM((rows, features), bf16),
+            pltpu.VMEM((rows, features), f32),
+            pltpu.VMEM((rows, features), f32),
+            pltpu.VMEM((3, rows, features), bf16),
+            pltpu.VMEM((3, rows, features), bf16),
+            pltpu.VMEM((2, rows, 3 * width), bf16),
+            pltpu.VMEM((rows, heads_width), bf16),
+            pltpu.VMEM((keys, pair_width), bf16),
+            pltpu.VMEM((rows, last_width), bf16),
+            pltpu.VMEM((keys, rows), f32),
+            pltpu.VMEM((HEAD_DIM, keys), bf16),
+            pltpu.VMEM((keys, HEAD_DIM), f32),
+            pltpu.VMEM((keys, HEAD_DIM), f32),
+            pltpu.VMEM((rows, heads_width), bf16),
+            pltpu.VMEM((keys - rows, pair_width), bf16),
+            pltpu.VMEM((3, rows, pair_width), bf16),
+            pltpu.VMEM((1, small_width), f32),
+            pltpu.VMEM((4, 1, small_width), f32),
+            pltpu.VMEM((4, 1, small_width), f32),
+            dma((3, size)),
+            dma((3, size)),
+            dma((units,)),
+            dma((3,)),
+            dma((3, units)),
+            dma((3, units)),
+            dma((count,)),
+            dma((count,)),
+            dma((count,)),
+            dma((count,)),
+            dma((2, 2)),
+            dma((count,)),
+            dma((size,)),
+            dma((4, size - 1)),
+            dma((4, size - 1)),
+            dma((3,)),
+            dma((3,)),
+            dma((3,)),
+            dma((3,)),
+            dma((size - 1,)),
+            dma((size - 1,)),
+            dma((3,)),
+            dma((3,)),
+            dma((3, size)),
+        ],
+        compiler_params=pltpu.CompilerParams(
+            collective_id=0, has_side_effects=True, vmem_limit_bytes=60 << 20
+        ),
+        name="layer_back",
+    )(
+        length, gains, lse, cosine, sine, hidden, tokens, grad_out, query, pair, mixed,
+        *feed_own, *feed_near, *far_flat, *out_pieces, *pair_pieces,
+    )
+    return results[:5]
+
+
 def chunk_edges(columns):
     tiles = columns // 128
     count = next((n for n in (7, 5, 4, 6, 3, 2) if tiles % n == 0), 1)
@@ -702,7 +1313,17 @@
     out_weights = gather_pieces(w_out, size, lanes, parity)
     edges = chunk_edges(unit_cols)
     feed_weights = []
-    early = len(edges) - 2
+    mega = (
+        size == 4
+        and blocks_along == 4
+        and lax.axis_size("tensor") == 2
+        and own_rows % 128 == 0
+        and row_count % 64 == 0
+        and len(set(w for _, w in edges)) == 1
+        and kv_count == 1
+        and seq_count == 1
+    )
+    early = len(edges) if mega else len(edges) - 2
 
     feed_own = (w_gate, w_up, w_down)
     feed_near = tuple(lax.ppermute(w, "dp", xor_pairs(size, 1)) for w in feed_own)
@@ -766,6 +1387,50 @@
     branch = absolute([branch[:, r * own_rows : (r + 1) * own_rows] for r in range(size)])
     hidden = inputs + tensor_sum(branch)
     scale_two = lax.rsqrt(jnp.mean(hidden * hidden, -1, keepdims=True) + EPSILON)
+    if mega:
+        gains = jnp.concatenate(
+            [jnp.concatenate(relative(g[None, :]), 1) for g in (gain_first, gain_second)], 0
+        )
+        output, grad_tokens, small, feed_sums, last_sums = layer_back(
+            lengths,
+            hidden,
+            tokens.reshape(row_count, model_width),
+            grad_out.reshape(row_count, model_width),
+            gains,
+            feed_own,
+            feed_near,
+            [(sources[2][0], sources[3][0]) for sources in feed_weights],
+            out_weights,
+            attention_weights,
+            query_rot,
+            pair_all,
+            lse,
+            mixed_heads,
+            cosine,
+            sine,
+        )
+        small = small[0]
+        feed_grads = [
+            jnp.concatenate([feed_sums[3 * n + w].astype(f32) for n in range(len(edges))], 1)
+            for w in range(3)
+        ]
+        last_grad = jnp.concatenate([last_sums[0], last_sums[1]], 1).astype(f32)
+        turned_at = query_cols + key_cols
+        at = 2 * model_width
+        return (
+            output.reshape(seq_count, block_len, model_width),
+            grad_tokens.reshape(seq_count, block_len, model_width),
+            small[:model_width],
+            last_grad[:, :query_cols],
+            small[at : at + query_cols],
+            last_grad[:, query_cols:turned_at],
+            small[at + query_cols : at + turned_at],
+            last_grad[:, turned_at : turned_at + key_cols],
+            small[at + turned_at :],
+            last_grad[:, turned_at + key_cols :],
+            small[model_width:at],
+            *feed_grads,
+        )
     normed_two = (hidden * scale_two * gain_second).astype(bf16)
     fall_grad = grad_out.reshape(row_count, model_width).astype(f32) * valid_rows
     fall_low = fall_grad.astype(bf16)

time: 727 us -> 606 us (0.83)
  local copies, waits for them, and re-layouts: 73.6 us -> 28.6 us
  other arithmetic: 78.2 us -> 34.5 us
  starting transfers between devices: 63.6 us -> 39.9 us
  waiting for transfers between devices: 114 us -> 95.1 us
  Pallas kernels: 379 us -> 394 us
    unnamed x250 -> x120, local copies, waits for them, and re-layouts: 33 us -> 11.1 us
    ppermute x20 -> x0, starting transfers between devices: 18 us -> none  [the longest x8 8.58 us: small_total(): vector = vector + lax.ppermute(vector, axis, xor_pairs(size, mask))]
    pallas_call x9 -> x1, Pallas kernels: 373 us -> 388 us  [layer_back(): pl.pallas_call(kernel, out_shape=(shape((rows, features), bf16), shape((r...]
    ppermute x4 -> x1, waiting for transfers between devices: 26.3 us -> 12.1 us  [tensor_sum(): other = lax.ppermute(sent, 'tensor', [(0, 1), (1, 0)])]
    ppermute x7, waiting for transfers between devices: 0.02 us -> 10.5 us  [fetch(): sources.append((lax.ppermute(far[r - 1], 'dp', xor_pairs(size, 1)),))]
    ppermute x20 -> x0, waiting for transfers between devices: 8.46 us -> none  [the longest x8 8.42 us: small_total(): vector = vector + lax.ppermute(vector, axis, xor_pairs(size, mask))]
    concatenate x11 -> x4, other arithmetic: 17.2 us -> 10.9 us  [the longest x3 10 us: local(): jnp.concatenate([feed_sums[3 * n + w].astype(f32) for n in range(len(edge...]
  transfers between devices with their start and end apart: 58 -> 35, of which waited for: 22 -> 21; matrix products, arithmetic and copies ran while one was open for 19% -> 6% of each run, Pallas kernels for 53% -> 1%
where the time goes in v3:
time: 606 us; the launch traced here: 600 us
  Pallas kernels  394 us (65%)
  waiting for transfers between devices  95.1 us (16%)
  starting transfers between devices  39.9 us (7%)
  other arithmetic  34.5 us (6%)
  local copies, waits for them, and re-layouts  28.6 us (5%)
    pallas_call x1, Pallas kernels, layer_back(): pl.pallas_call(kernel, out_shape=(shape((rows, features), bf16), shape((r...  388 us
    ppermute x17, waiting for transfers between devices, send(): got = lax.ppermute(array, axis, pairs)  72.4 us
    ppermute x17, starting transfers between devices, send(): got = lax.ppermute(array, axis, pairs)  24 us
  transfers between devices with their start and end apart: 35, of which 21 were waited for; matrix products, arithmetic and copies ran while one was open for 6% of the time, Pallas kernels for 1%

profile of v3, /device:TPU:0, one launch (start us, length us, event | category | flops | bytes accessed | tf_op | source)
XLA Modules:
  0.0 599.5 jit_solution(17162166729006155543)
XLA Ops:
  3.7 3.0 collective-permute-start.1
  8.7 3.2 fusion.39
  21.9 2.4 collective-permute-done.1.refs_37_
  26.7 5.9 collective-permute-done.7
  41.9 7.8 %collective-permute-done.14 = bf16[192,1920]{1,0:T(8,128)(2,1)} collective-permute-done((bf16[192,1920]{1,0:T(8,128)(2,1)}, bf16[192,1920]{1,0:T(8,128)(2,1)}, u32[]{:S(2)}, u32[]{:S(2)}) %collective-permute-start.14) | collective-permute-done | bytes 737312 | tf_op jit(solution)/shard_map/ppermute | solution.py:29
  52.4 2.5 fusion.11
  57.7 8.6 %collective-permute-done.17 = bf16[192,1920]{1,0:T(8,128)(2,1)} collective-permute-done((bf16[192,1920]{1,0:T(8,128)(2,1)}, bf16[192,1920]{1,0:T(8,128)(2,1)}, u32[]{:S(2)}, u32[]{:S(2)}) %collective-permute-start.17) | collective-permute-done | bytes 737312 | tf_op jit(solution)/shard_map/ppermute | solution.py:29
  71.3 5.7 collective-permute-start.5
  82.1 3.2 collective-permute-start.3
  91.2 5.7 attend.1
  98.1 2.8 collective-permute-done.23
  101.0 3.2 collective-permute-done.21
  104.2 2.5 collective-permute-start.24
  108.1 2.5 fusion.41
  110.8 12.5 %collective-permute-done.26 = bf16[192,1920]{1,0:T(8,128)(2,1)S(1)} collective-permute-done((bf16[192,1920]{1,0:T(8,128)(2,1)S(1)}, bf16[192,1920]{1,0:T(8,128)(2,1)S(1)}, u32[]{:S(2)}, u32[]{:S(2)}) %collective-permute-start.26) | collective-permute-done | bytes 737312 | tf_op jit(solution)/shard_map/ppermute | solution.py:29
  126.3 13.0 %collective-permute-done.29 = bf16[192,1920]{1,0:T(8,128)(2,1)S(1)} collective-permute-done((bf16[192,1920]{1,0:T(8,128)(2,1)S(1)}, bf16[192,1920]{1,0:T(8,128)(2,1)S(1)}, u32[]{:S(2)}, u32[]{:S(2)}) %collective-permute-start.29) | collective-permute-done | bytes 737312 | tf_op jit(solution)/shard_map/ppermute | solution.py:29
  143.2 11.8 %collective-permute-done.30 = bf16[192,1920]{1,0:T(8,128)(2,1)S(1)} collective-permute-done((bf16[192,1920]{1,0:T(8,128)(2,1)S(1)}, bf16[192,1920]{1,0:T(8,128)(2,1)S(1)}, u32[]{:S(2)}, u32[]{:S(2)}) %collective-permute-start.30) | collective-permute-done | bytes 737312 | tf_op jit(solution)/shard_map/ppermute | solution.py:29
  155.0 2.6 collective-permute-start.10
  158.1 12.1 %collective-permute-done.10 = bf16[256,1536]{1,0:T(8,128)(2,1)S(1)} collective-permute-done((bf16[256,1536]{1,0:T(8,128)(2,1)S(1)}, bf16[256,1536]{1,0:T(8,128)(2,1)S(1)}, u32[]{:S(2)}, u32[]{:S(2)}) %collective-permute-start.10) | collective-permute-done | bytes 786464 | tf_op jit(solution)/shard_map/ppermute | solution.py:89
  179.7 2.1 collective-permute-done.28.refs_26_
  187.3 388.4 %layer_back.1 = (bf16[256,1536]{1,0:T(8,128)(2,1)}, bf16[256,1536]{1,0:T(8,128)(2,1)}, f32[1,4096]{1,0:T(1,128)}, bf16[21,384,640]{2,1,0:T(8,128)(2,1)}, bf16[2,...) custom-call(s32[1]{0:T(128)S(6)} %copy.60.refs_0_, ...), custom_call_target="tpu_custom_call" | custom-call | tf_op jit(solution)/shard_map/layer_back/pallas_call | solution.py:1174
  587.6 3.3 concatenate.149
  590.9 3.3 concatenate.147
  594.2 3.3 concatenate.145
  (243 shorter events, 85.5 us)
Async XLA Ops:
  3.7 20.7 %collective-permute-start.1 = (bf16[384,1024]{1,0:T(8,128)(2,1)S(1)}, bf16[384,1024]{1,0:T(8,128)(2,1)}, u32[]{:S(2)}, u32[]{:S(2)}) collective-permute-start(bf16[384,1024]{1,0:T(8,128)(2,1)S(1)} %constant_dynamic-update-slice_fusion.refs_35_), channel_id=1, source_target_pairs={{0,16},{8,24},{16,0},{24,8},{1,17},{9,25},{17,1},{25,9},{2,18},{10... | collective-permute-start | bytes 2359304 | tf_op jit(solution)/shard_map/ppermute | solution.py:29
  6.7 45.6 %collective-permute-start = (bf16[384,1024]{1,0:T(8,128)(2,1)S(1)}, bf16[384,1024]{1,0:T(8,128)(2,1)}, u32[]{:S(2)}, u32[]{:S(2)}) collective-permute-start(bf16[384,1024]{1,0:T(8,128)(2,1)S(1)} %constant_dynamic-update-slice_fusion.refs_35_), channel_id=1, source_target_pairs={{0,8},{8,0},{16,24},{24,16},{1,9},{9,1},{17,25},{25,17},{2,10},{10... | collective-permute-start | bytes 2359304 | tf_op jit(solution)/shard_map/ppermute | solution.py:75
  6.7 31.3 %collective-permute-start.6 = (bf16[384,768]{1,0:T(8,128)(2,1)}, bf16[384,768]{1,0:T(8,128)(2,1)}, u32[]{:S(2)}, u32[]{:S(2)}) collective-permute-start(bf16[384,768]{1,0:T(8,128)(2,1)} %refs_31_.1), channel_id=1, source_target_pairs={{0,8},{8,0},{16,24},{24,16},{1,9},{9,1},{17,25},{25,17},{2,10},{10... | collective-permute-start | bytes 1769480 | tf_op jit(solution)/shard_map/ppermute | solution.py:75
  26.1 26.2 %collective-permute-start.2 = (bf16[384,1024]{1,0:T(8,128)(2,1)}, bf16[384,1024]{1,0:T(8,128)(2,1)}, u32[]{:S(2)}, u32[]{:S(2)}) collective-permute-start(bf16[384,1024]{1,0:T(8,128)(2,1)} %collective-permute-done.1.refs_37_), channel_id=1, source_target_pairs={{0,8},{8,0},{16,24},{24,16},{1,9},{9,1},{17,25},{25,17},{2,10},{10... | collective-permute-start | bytes 2359304 | tf_op jit(solution)/shard_map/ppermute | solution.py:75
  32.6 17.1 %collective-permute-start.14 = (bf16[192,1920]{1,0:T(8,128)(2,1)}, bf16[192,1920]{1,0:T(8,128)(2,1)}, u32[]{:S(2)}, u32[]{:S(2)}) collective-permute-start(bf16[192,1920]{1,0:T(8,128)(2,1)} %fusion.34), channel_id=1, source_target_pairs={{0,16},{8,24},{16,0},{24,8},{1,17},{9,25},{17,1},{25,9},{2,18},{10... | collective-permute-start | bytes 2211848 | tf_op jit(solution)/shard_map/ppermute | solution.py:29
  49.6 16.7 %collective-permute-start.15 = (bf16[192,1920]{1,0:T(8,128)(2,1)}, bf16[192,1920]{1,0:T(8,128)(2,1)}, u32[]{:S(2)}, u32[]{:S(2)}) collective-permute-start(bf16[192,1920]{1,0:T(8,128)(2,1)} %collective-permute-done.14), channel_id=1, source_target_pairs={{0,2},{2,0},{4,6},{6,4},{1,3},{3,1},{5,7},{7,5},{8,10},{10,8},{12,... | collective-permute-start | bytes 2211848 | tf_op jit(solution)/shard_map/ppermute | solution.py:29
  50.8 15.5 %collective-permute-start.17 = (bf16[192,1920]{1,0:T(8,128)(2,1)}, bf16[192,1920]{1,0:T(8,128)(2,1)}, u32[]{:S(2)}, u32[]{:S(2)}) collective-permute-start(bf16[192,1920]{1,0:T(8,128)(2,1)} %fusion.32), channel_id=1, source_target_pairs={{0,16},{8,24},{16,0},{24,8},{1,17},{9,25},{17,1},{25,9},{2,18},{10... | collective-permute-start | bytes 2211848 | tf_op jit(solution)/shard_map/ppermute | solution.py:29
  66.4 18.9 %collective-permute-start.18 = (bf16[192,1920]{1,0:T(8,128)(2,1)}, bf16[192,1920]{1,0:T(8,128)(2,1)S(1)}, u32[]{:S(2)}, u32[]{:S(2)}) collective-permute-start(bf16[192,1920]{1,0:T(8,128)(2,1)} %collective-permute-done.17), channel_id=1, source_target_pairs={{0,2},{2,0},{4,6},{6,4},{1,3},{3,1},{5,7},{7,5},{8,10},{10,8},{12,... | collective-permute-start | bytes 2211848 | tf_op jit(solution)/shard_map/ppermute | solution.py:29
  68.0 14.1 %collective-permute-start.20 = (bf16[192,1920]{1,0:T(8,128)(2,1)}, bf16[192,1920]{1,0:T(8,128)(2,1)S(1)}, u32[]{:S(2)}, u32[]{:S(2)}) collective-permute-start(bf16[192,1920]{1,0:T(8,128)(2,1)} %fusion.30), channel_id=1, source_target_pairs={{0,16},{8,24},{16,0},{24,8},{1,17},{9,25},{17,1},{25,9},{2,18},{10... | collective-permute-start | bytes 2211848 | tf_op jit(solution)/shard_map/ppermute | solution.py:29
  71.3 16.1 %collective-permute-start.5 = (bf16[256,256]{1,0:T(8,128)(2,1)S(1)}, bf16[256,256]{1,0:T(8,128)(2,1)S(1)}, u32[]{:S(2)}, u32[]{:S(2)}) collective-permute-start(bf16[256,256]{1,0:T(8,128)(2,1)S(1)} %pad_maximum_fusion.12), channel_id=1, source_target_pairs={{0,6},{1,7},{8,14},{9,15},{16,22},{17,23},{24,30},{25,31}} | collective-permute-start | bytes 393224 | tf_op jit(solution)/shard_map/ppermute | solution.py:1379
  78.8 18.2 %collective-permute-start.9 = (bf16[384,768]{1,0:T(8,128)(2,1)S(1)}, bf16[384,768]{1,0:T(8,128)(2,1)S(1)}, u32[]{:S(2)}, u32[]{:S(2)}) collective-permute-start(bf16[384,768]{1,0:T(8,128)(2,1)S(1)} %pad_maximum_fusion.8.refs_33_), channel_id=1, source_target_pairs={{0,8},{8,0},{16,24},{24,16},{1,9},{9,1},{17,25},{25,17},{2,10},{10... | collective-permute-start | bytes 1769480 | tf_op jit(solution)/shard_map/ppermute | solution.py:75
  85.3 18.8 %collective-permute-start.21 = (bf16[192,1920]{1,0:T(8,128)(2,1)S(1)}, bf16[192,1920]{1,0:T(8,128)(2,1)S(1)}, u32[]{:S(2)}, u32[]{:S(2)}) collective-permute-start(bf16[192,1920]{1,0:T(8,128)(2,1)S(1)} %collective-permute-done.20), channel_id=1, source_target_pairs={{0,2},{2,0},{4,6},{6,4},{1,3},{3,1},{5,7},{7,5},{8,10},{10,8},{12,... | collective-permute-start | bytes 2211848 | tf_op jit(solution)/shard_map/ppermute | solution.py:29
  87.4 13.6 %collective-permute-start.23 = (bf16[192,1920]{1,0:T(8,128)(2,1)}, bf16[192,1920]{1,0:T(8,128)(2,1)S(1)}, u32[]{:S(2)}, u32[]{:S(2)}) collective-permute-start(bf16[192,1920]{1,0:T(8,128)(2,1)} %fusion.28), channel_id=1, source_target_pairs={{0,16},{8,24},{16,0},{24,8},{1,17},{9,25},{17,1},{25,9},{2,18},{10... | collective-permute-start | bytes 2211848 | tf_op jit(solution)/shard_map/ppermute | solution.py:29
  89.7 81.7 %collective-permute-start.11 = (bf16[384,4480]{1,0:T(8,128)(2,1)S(1)}, bf16[384,4480]{1,0:T(8,128)(2,1)}, u32[]{:S(2)}, u32[]{:S(2)}) collective-permute-start(bf16[384,4480]{1,0:T(8,128)(2,1)S(1)} %copy-done.4), channel_id=1, source_target_pairs={{0,8},{8,0},{16,24},{24,16},{1,9},{9,1},{17,25},{25,17},{2,10},{10... | collective-permute-start | bytes 10321928 | tf_op jit(solution)/shard_map/ppermute | solution.py:1329
  89.9 82.1 %collective-permute-start.12 = (bf16[384,4480]{1,0:T(8,128)(2,1)S(1)}, bf16[384,4480]{1,0:T(8,128)(2,1)}, u32[]{:S(2)}, u32[]{:S(2)}) collective-permute-start(bf16[384,4480]{1,0:T(8,128)(2,1)S(1)} %copy-done.6), channel_id=1, source_target_pairs={{0,8},{8,0},{16,24},{24,16},{1,9},{9,1},{17,25},{25,17},{2,10},{10... | collective-permute-start | bytes 10321928 | tf_op jit(solution)/shard_map/ppermute | solution.py:1329
  97.0 75.6 %collective-permute-start.13 = (bf16[384,4480]{1,0:T(8,128)(2,1)S(1)}, bf16[384,4480]{1,0:T(8,128)(2,1)S(1)}, u32[]{:S(2)}, u32[]{:S(2)}) collective-permute-start(bf16[384,4480]{1,0:T(8,128)(2,1)S(1)} %copy-done.8), channel_id=1, source_target_pairs={{0,8},{8,0},{16,24},{24,16},{1,9},{9,1},{17,25},{25,17},{2,10},{10... | collective-permute-start | bytes 10321928 | tf_op jit(solution)/shard_map/ppermute | solution.py:1329
  104.2 19.1 %collective-permute-start.24 = (bf16[192,1920]{1,0:T(8,128)(2,1)S(1)}, bf16[192,1920]{1,0:T(8,128)(2,1)S(1)}, u32[]{:S(2)}, u32[]{:S(2)}) collective-permute-start(bf16[192,1920]{1,0:T(8,128)(2,1)S(1)} %collective-permute-done.23), channel_id=1, source_target_pairs={{0,2},{2,0},{4,6},{6,4},{1,3},{3,1},{5,7},{7,5},{8,10},{10,8},{12,... | collective-permute-start | bytes 2211848 | tf_op jit(solution)/shard_map/ppermute | solution.py:29
  106.7 16.6 %collective-permute-start.26 = (bf16[192,1920]{1,0:T(8,128)(2,1)S(1)}, bf16[192,1920]{1,0:T(8,128)(2,1)S(1)}, u32[]{:S(2)}, u32[]{:S(2)}) collective-permute-start(bf16[192,1920]{1,0:T(8,128)(2,1)S(1)} %copy-done.43), channel_id=1, source_target_pairs={{0,16},{8,24},{16,0},{24,8},{1,17},{9,25},{17,1},{25,9},{2,18},{10... | collective-permute-start | bytes 2211848 | tf_op jit(solution)/shard_map/ppermute | solution.py:29
  123.3 16.4 %collective-permute-start.27 = (bf16[192,1920]{1,0:T(8,128)(2,1)S(1)}, bf16[192,1920]{1,0:T(8,128)(2,1)S(1)}, u32[]{:S(2)}, u32[]{:S(2)}) collective-permute-start(bf16[192,1920]{1,0:T(8,128)(2,1)S(1)} %collective-permute-done.26), channel_id=1, source_target_pairs={{0,2},{2,0},{4,6},{6,4},{1,3},{3,1},{5,7},{7,5},{8,10},{10,8},{12,... | collective-permute-start | bytes 2211848 | tf_op jit(solution)/shard_map/ppermute | solution.py:29
  123.6 15.7 %collective-permute-start.29 = (bf16[192,1920]{1,0:T(8,128)(2,1)S(1)}, bf16[192,1920]{1,0:T(8,128)(2,1)S(1)}, u32[]{:S(2)}, u32[]{:S(2)}) collective-permute-start(bf16[192,1920]{1,0:T(8,128)(2,1)S(1)} %fusion.24), channel_id=1, source_target_pairs={{0,16},{8,24},{16,0},{24,8},{1,17},{9,25},{17,1},{25,9},{2,18},{10... | collective-permute-start | bytes 2211848 | tf_op jit(solution)/shard_map/ppermute | solution.py:29
  139.7 15.4 %collective-permute-start.30 = (bf16[192,1920]{1,0:T(8,128)(2,1)S(1)}, bf16[192,1920]{1,0:T(8,128)(2,1)S(1)}, u32[]{:S(2)}, u32[]{:S(2)}) collective-permute-start(bf16[192,1920]{1,0:T(8,128)(2,1)S(1)} %collective-permute-done.29), channel_id=1, source_target_pairs={{0,2},{2,0},{4,6},{6,4},{1,3},{3,1},{5,7},{7,5},{8,10},{10,8},{12,... | collective-permute-start | bytes 2211848 | tf_op jit(solution)/shard_map/ppermute | solution.py:29
  141.4 16.2 %collective-permute-start.32 = (bf16[192,1920]{1,0:T(8,128)(2,1)S(1)}, bf16[192,1920]{1,0:T(8,128)(2,1)S(1)}, u32[]{:S(2)}, u32[]{:S(2)}) collective-permute-start(bf16[192,1920]{1,0:T(8,128)(2,1)S(1)} %copy-done.42), channel_id=1, source_target_pairs={{0,16},{8,24},{16,0},{24,8},{1,17},{9,25},{17,1},{25,9},{2,18},{10... | collective-permute-start | bytes 2211848 | tf_op jit(solution)/shard_map/ppermute | solution.py:29
  155.0 15.1 %collective-permute-start.10 = (bf16[256,1536]{1,0:T(8,128)(2,1)S(1)}, bf16[256,1536]{1,0:T(8,128)(2,1)S(1)}, u32[]{:S(2)}, u32[]{:S(2)}) collective-permute-start(bf16[256,1536]{1,0:T(8,128)(2,1)S(1)} %pad_maximum_fusion.7), channel_id=1, source_target_pairs={{0,1},{1,0},{2,3},{3,2},{4,5},{5,4},{6,7},{7,6},{8,9},{9,8},{10,11... | collective-permute-start | bytes 2359304 | tf_op jit(solution)/shard_map/ppermute | solution.py:89
  157.7 13.0 %collective-permute-start.33 = (bf16[192,1920]{1,0:T(8,128)(2,1)S(1)}, bf16[192,1920]{1,0:T(8,128)(2,1)S(1)}, u32[]{:S(2)}, u32[]{:S(2)}) collective-permute-start(bf16[192,1920]{1,0:T(8,128)(2,1)S(1)} %collective-permute-done.32), channel_id=1, source_target_pairs={{0,2},{2,0},{4,6},{6,4},{1,3},{3,1},{5,7},{7,5},{8,10},{10,8},{12,... | collective-permute-start | bytes 2211848 | tf_op jit(solution)/shard_map/ppermute | solution.py:29
  (65 other events, 766.8 us)
